TPU v7x, 128 devices: a whole 4x4x4 slice. The times are simulated.
128 devices in a mesh: sec: 2 (over y_hi), dev: 32 (over z, x, core), tp: 2 (over y_lo).
Axes of the slice: x: 4, y: 4 (y_hi: 2, y_lo: 2; y = y_hi * 2 + y_lo), z: 4, core: 2. Of those that a mesh axis runs over, the one named last changes fastest.
Arguments:
- queries: bfloat16 [512, 8192], P(('sec', 'dev'), 'tp'), may hold values from -6 to 6
- new_keys: bfloat16 [512, 1024], P(('sec', 'dev'), 'tp'), may hold values from -6 to 6
- token_values: bfloat16 [512, 1024], P(('sec', 'dev'), 'tp'), may hold values from -6 to 6
- key_cache: bfloat16 [512, 256, 1024], P(('sec', 'dev'), None, 'tp'), may hold values from -6 to 6
- stored_values: bfloat16 [512, 256, 1024], P(('sec', 'dev'), None, 'tp'), may hold values from -6 to 6
- cache_lengths: int32 [512], P(('sec', 'dev')), may hold values from 1 to 256, 65536 in all
- residual: bfloat16 [512, 8192], P(('sec', 'dev', 'tp')), may hold values from -6 to 6
- norm_gain: float32 [8192], replicated, may hold values from 0.25 to 1.75
- active: int32 [512, 16], P(('sec', 'dev', 'tp')), may hold values from 0 to 127, all different within a row; in each aligned block of 4 rows (0 to 3, 4 to 7, ...) at most 3 rows name the same one
- gate_weight: bfloat16 [8192, 16384], P(None, ('sec', 'dev', 'tp')), may hold values from -0.0625 to 0.0625
- up_weight: bfloat16 [8192, 16384], P(None, ('sec', 'dev', 'tp')), may hold values from -0.0625 to 0.0625
- down_weight: bfloat16 [16384, 8192], P(('sec', 'dev', 'tp')), may hold values from -0.125 to 0.125
Outputs:
- layer_out: bfloat16 [512, 8192], P(('sec', 'dev', 'tp'))
Inputs may be any that keep to these rules, and one draw needn't show every extreme that they name: `cache_lengths`: the largest length is 256 in every draw. `active`: the bundles of one row are distinct. Among the 4 rows of one device (aligned blocks of rows), no bundle is named by more than 3 rows, and some bundle reaches 3.
All inputs are finite; a program needn't handle non-finite values. No bound on the sum of `cache_lengths` on one device may be relied on, other than what follows from the above.
Results may differ from a plain program's by a relative error of at most 0.007.
Values may be sent and summed in bfloat16 or wider, within the bound.
A program may use at most 128 MiB of HBM per device.

v0:
```python
import jax
import jax.numpy as jnp
from jax import lax
from jax.sharding import PartitionSpec as P

HEAD_SIZE = 128
CACHE_POSITIONS = 256


epsilon = 1e-05


def attend(queries, new_keys, token_values, key_cache, stored_values, cache_lengths):
    request_count, query_width = queries.shape
    kv_width = new_keys.shape[1]
    kv_heads = kv_width // HEAD_SIZE
    group_width = query_width // kv_width
    scaling = HEAD_SIZE ** (-0.5)
    grouped = queries.reshape(request_count, kv_heads, group_width, HEAD_SIZE)
    cached_keys = key_cache.reshape(request_count, CACHE_POSITIONS, kv_heads, HEAD_SIZE)
    cached_values = stored_values.reshape(request_count, CACHE_POSITIONS, kv_heads, HEAD_SIZE)
    scores = (
        jnp.einsum("rkgd,rckd->rkgc", grouped, cached_keys, preferred_element_type=jnp.float32)
        * scaling
    )
    visible = jnp.arange(CACHE_POSITIONS, dtype=jnp.int32)[None, :] < cache_lengths[:, None]
    scores = jnp.where(visible[:, None, None, :], scores, -jnp.inf)
    fresh_keys = new_keys.reshape(request_count, kv_heads, HEAD_SIZE)
    fresh_score = (
        jnp.einsum("rkgd,rkd->rkg", grouped, fresh_keys, preferred_element_type=jnp.float32)
        * scaling
    )
    highest = jnp.maximum(jnp.max(scores, axis=-1), fresh_score)
    weights_cache = jnp.exp(scores - highest[..., None])
    weight_fresh = jnp.exp(fresh_score - highest)
    denominator = jnp.sum(weights_cache, axis=-1) + weight_fresh
    probs_cache = (weights_cache / denominator[..., None]).astype(jnp.bfloat16)
    prob_fresh = (weight_fresh / denominator).astype(jnp.bfloat16)
    blended = jnp.einsum(
        "rkgc,rckd->rkgd", probs_cache, cached_values, preferred_element_type=jnp.float32
    )
    fresh_values = token_values.reshape(request_count, kv_heads, 1, HEAD_SIZE).astype(jnp.float32)
    blended = blended + prob_fresh[..., None].astype(jnp.float32) * fresh_values
    return blended.reshape(request_count, query_width).astype(jnp.bfloat16)


def feed_forward(row_block, gate_weight, up_weight, selected):
    gate_value = jnp.dot(row_block, gate_weight, preferred_element_type=jnp.float32)
    up_value = jnp.dot(row_block, up_weight, preferred_element_type=jnp.float32)
    return (jax.nn.relu(gate_value) * up_value * selected).astype(jnp.bfloat16)


def shards(
    queries,
    new_keys,
    token_values,
    key_cache,
    stored_values,
    cache_lengths,
    residual,
    norm_gain,
    active,
    gate_weight,
    up_weight,
    down_weight,
):
    context = attend(queries, new_keys, token_values, key_cache, stored_values, cache_lengths)
    context = lax.all_to_all(context, "tp", split_axis=0, concat_axis=1, tiled=True)
    stream = residual.astype(jnp.float32) + context.astype(jnp.float32)
    mean_square = jnp.mean(stream * stream, axis=1, keepdims=True)
    normed = (stream * lax.rsqrt(mean_square + epsilon) * norm_gain[None, :]).astype(jnp.bfloat16)
    local_rows, model_width = normed.shape
    device_count = lax.axis_size(("sec", "dev", "tp"))
    top_count = active.shape[1]
    slot_limit = max(3, (2 * local_rows * top_count + device_count - 1) // device_count)
    targets = jnp.arange(device_count, dtype=jnp.int32)
    naming = jnp.any(active[:, :, None] == targets[None, None, :], axis=1).astype(jnp.int32)
    earlier = jnp.cumsum(naming, axis=0) - naming
    slot_ids = jnp.arange(slot_limit, dtype=jnp.int32)
    placed = (
        (naming.T[:, None, :] == 1) & (earlier.T[:, None, :] == slot_ids[None, :, None])
    ).astype(jnp.bfloat16)
    outgoing = jnp.einsum("bsr,rd->bsd", placed, normed, preferred_element_type=jnp.float32).astype(
        jnp.bfloat16
    )
    received = lax.all_to_all(
        outgoing, ("sec", "dev", "tp"), split_axis=0, concat_axis=0, tiled=True
    )
    slot_count = received.shape[1]
    flat_rows = received.reshape(device_count * slot_count, model_width)
    hidden = feed_forward(flat_rows, gate_weight, up_weight, 1.0)
    partial_terms = jnp.dot(hidden, down_weight, preferred_element_type=jnp.float32)
    partial_terms = partial_terms.reshape(device_count, slot_count, model_width)
    returned = lax.all_to_all(
        partial_terms.astype(jnp.bfloat16),
        ("sec", "dev", "tp"),
        split_axis=0,
        concat_axis=0,
        tiled=True,
    ).astype(partial_terms.dtype)
    update = jnp.einsum(
        "bsr,bsd->rd", placed.astype(jnp.float32), returned, precision=lax.Precision.HIGHEST
    )
    return (stream + update).astype(jnp.bfloat16)


def solution(mesh):
    return jax.shard_map(
        shards,
        mesh=mesh,
        in_specs=(
            P(("sec", "dev"), "tp"),
            P(("sec", "dev"), "tp"),
            P(("sec", "dev"), "tp"),
            P(("sec", "dev"), None, "tp"),
            P(("sec", "dev"), None, "tp"),
            P(("sec", "dev")),
            P(("sec", "dev", "tp"), None),
            P(),
            P(("sec", "dev", "tp"), None),
            P(None, ("sec", "dev", "tp")),
            P(None, ("sec", "dev", "tp")),
            P(("sec", "dev", "tp"), None),
        ),
        out_specs=P(("sec", "dev", "tp"), None),
        check_vma=False,
    )
```

profile of v0, /device:TPU:0, one launch (start us, length us, event | category | flops | bytes accessed | tf_op | source)
XLA Modules:
  0.0 297.7 jit_solution(82121312440829299)
XLA Ops:
  0.0 0.0 copy-start
  0.0 0.0 copy-start.4
  0.0 0.9 iota_compare_fusion.1
  0.9 0.8 bitcast_convert_fusion
  1.7 1.0 fusion.29
  2.7 2.4 fusion.43
  5.1 0.0 copy-start.3
  5.1 0.2 fusion.22
  5.3 0.0 copy-start.1
  5.4 0.0 copy-done.4
  5.4 0.0 copy-start.2
  5.4 0.5 fusion.19
  5.8 0.7 convert_element_type.74
  6.5 3.3 %all-to-all-start = ((bf16[2,4,4096]{2,1,0:T(4,128)(2,1)}), bf16[2,4,4096]{2,1,0:T(4,128)(2,1)S(1)}, u32[]{:S(2)}, u32[]{:S(2)}) async-start(bf16[2,4,4096]{2,1,0:T(4,128)(2,1)} %convert_element_type.74), calls=%async_computation | async-start | bytes 131072 | tf_op jit(solution)/shard_map/all_to_all | solution.py:68
  9.8 0.0 copy-done.3
  9.8 0.1 fusion.32
  10.0 3.9 %all-to-all-done = bf16[2,4,4096]{2,1,0:T(4,128)(2,1)S(1)} async-done(((bf16[2,4,4096]{2,1,0:T(4,128)(2,1)}), bf16[2,4,4096]{2,1,0:T(4,128)(2,1)S(1)}, u32[]{:S(2)}, u32[]{:S(2)}) %all-to-all-start) | async-done | bytes 65568 | tf_op jit(solution)/shard_map/all_to_all | solution.py:68
  13.9 0.0 copy-done.1
  13.9 0.2 multiply_reduce_fusion
  14.1 0.0 copy-done.2
  14.1 4.6 %convolution_convert_fusion.1 = bf16[128,3,8192]{2,0,1:T(8,128)(2,1)} fusion(f32[8192]{0:T(1024)S(1)} %copy-done.2, f32[4]{0:T(128)S(1)} %add_rsqrt_fusion, f32[4,8192]{1,0:T(4,128)S(1)} %bitcast.57, bf16[4,8192]{1,0:T(4,128)(2,1)S(1)} %copy-done.1, s32[128,4]{0,1:T(4,128)S(1)} %subtract_bitcast_fusion, pred[128,4]{0,1:T(4,128)(4,1)S(1)} %get-tuple-element.7), kind=kOutput, calls=%fused_computation.1 | convolution fusion | flops 28478464 | bytes 6523408 | tf_op jit(solution)/shard_map/bsr,rd->bsd/dot_general | solution.py:83
  18.7 11.4 %copy.34 = bf16[128,3,8192]{2,1,0:T(4,128)(2,1)} copy(bf16[128,3,8192]{2,0,1:T(8,128)(2,1)} %convolution_convert_fusion.1) | data formatting | bytes 12582912 | tf_op jit(solution)/shard_map/convert_element_type | solution.py:83
  30.1 109.0 %all_to_all.20 = bf16[128,3,8192]{2,1,0:T(4,128)(2,1)} all-to-all(bf16[128,3,8192]{2,1,0:T(4,128)(2,1)} %copy.34), channel_id=1, replica_groups=mesh['sec'=2,'dev'=32,'tp'=2] {'sec','dev','tp'}, dimensions={0} | all-to-all | bytes 12582912 | tf_op jit(solution)/shard_map/all_to_all | solution.py:86
  139.1 13.7 %reshape.73 = bf16[384,8192]{1,0:T(8,128)(2,1)} reshape(bf16[128,3,8192]{2,1,0:T(4,128)(2,1)} %all_to_all.20) | data formatting | bytes 12582912 | tf_op jit(solution)/shard_map/reshape | solution.py:90
  152.8 5.2 %convolution_maximum_fusion = f32[384,128]{1,0:T(8,128)S(1)} fusion(bf16[384,8192]{1,0:T(8,128)(2,1)} %reshape.73, bf16[8192,128]{1,0:T(8,128)(2,1)} %param.21), kind=kOutput, calls=%fused_computation.15 | convolution fusion | flops 805355520 | bytes 8585216 | tf_op jit(solution)/shard_map/dot_general | solution.py:48
  158.0 0.0 copy-done
  158.0 12.8 %convolution_convert_fusion = bf16[384,8192]{1,0:T(8,128)(2,1)} fusion(bf16[128,8192]{1,0:T(8,128)(2,1)S(1)} %copy-done, f32[384,128]{1,0:T(8,128)S(1)} %convolution_maximum_fusion, bf16[384,8192]{1,0:T(8,128)(2,1)} %reshape.73, bf16[8192,128]{1,0:T(8,128)(2,1)} %param.22), kind=kOutput, calls=%fused_computation | convolution fusion | flops 1613856768 | bytes 16973824 | tf_op jit(solution)/shard_map/dot_general | solution.py:92
  170.8 12.8 %convert_element_type.83 = bf16[128,3,8192]{2,1,0:T(4,128)(2,1)} reshape(bf16[384,8192]{1,0:T(8,128)(2,1)} %convolution_convert_fusion) | data formatting | bytes 12582912 | tf_op jit(solution)/shard_map/convert_element_type | solution.py:95
  183.6 106.7 %all_to_all.21 = bf16[128,3,8192]{2,1,0:T(4,128)(2,1)S(1)} all-to-all(bf16[128,3,8192]{2,1,0:T(4,128)(2,1)} %convert_element_type.83), channel_id=1, replica_groups=mesh['sec'=2,'dev'=32,'tp'=2] {'sec','dev','tp'}, dimensions={0} | all-to-all | bytes 12582912 | tf_op jit(solution)/shard_map/all_to_all | solution.py:94
  290.4 7.3 %fusion.1 = bf16[4,8192]{1,0:T(4,128)(2,1)} fusion(bf16[128,3,8192]{2,1,0:T(4,128)(2,1)S(1)} %all_to_all.21, f32[4,8192]{1,0:T(4,128)S(1)} %bitcast.58, bf16[4,8192]{1,0:T(4,128)(2,1)S(1)} %copy-done.1, s32[128,4]{0,1:T(4,128)S(1)} %subtract_bitcast_fusion, pred[128,4]{0,1:T(4,128)(4,1)S(1)} %get-tuple-element.7), kind=kOutput, calls=%fused_computation.4 | convolution fusion | flops 25299968 | bytes 6556160 | tf_op jit(solution)/shard_map/bsr,bsd->rd/dot_general | solution.py:101
  (8 shorter events, 0.1 us)
Async XLA Ops:
  0.0 158.0 %copy-start = (bf16[128,8192]{1,0:T(8,128)(2,1)S(1)}, bf16[128,8192]{1,0:T(8,128)(2,1)}, u32[]{:S(2)}) copy-start(bf16[128,8192]{1,0:T(8,128)(2,1)} %param.23) | copy-start | bytes 6291460
  0.0 5.4 %copy-start.4 = (bf16[8,256,512]{2,1,0:T(8,128)(2,1)S(1)}, bf16[8,256,512]{2,1,0:T(8,128)(2,1)}, u32[]{:S(2)}) copy-start(bf16[8,256,512]{2,1,0:T(8,128)(2,1)} %param.16) | copy-start | bytes 6291460
  5.1 4.7 %copy-start.3 = (s32[4,16]{1,0:T(4,128)S(1)}, s32[4,16]{1,0:T(4,128)}, u32[]{:S(2)}) copy-start(s32[4,16]{1,0:T(4,128)} %param.20) | copy-start | bytes 772
  5.3 8.6 %copy-start.1 = (bf16[4,8192]{1,0:T(4,128)(2,1)S(1)}, bf16[4,8192]{1,0:T(4,128)(2,1)}, u32[]{:S(2)}) copy-start(bf16[4,8192]{1,0:T(4,128)(2,1)} %param.18) | copy-start | bytes 196612
  5.4 8.8 %copy-start.2 = (f32[8192]{0:T(1024)S(1)}, f32[8192]{0:T(1024)}, u32[]{:S(2)}) copy-start(f32[8192]{0:T(1024)} %param.19) | copy-start | bytes 98308
  6.5 7.4 %all-to-all-start = ((bf16[2,4,4096]{2,1,0:T(4,128)(2,1)}), bf16[2,4,4096]{2,1,0:T(4,128)(2,1)S(1)}, u32[]{:S(2)}, u32[]{:S(2)}) async-start(bf16[2,4,4096]{2,1,0:T(4,128)(2,1)} %convert_element_type.74), calls=%async_computation | async-start | bytes 131072 | tf_op jit(solution)/shard_map/all_to_all | solution.py:68
where the time goes:
time: 302 us; the launch traced here: 298 us
  blocking collectives  216 us (72%)
  local copies, waits for them, and re-layouts  38.6 us (13%)
  matrix products  33.7 us (11%)
  waiting for transfers between devices  3.94 us (1%)
  starting transfers between devices  3.3 us (1%)
    all_to_all x1, blocking collectives, shards(): lax.all_to_all(outgoing, ('sec', 'dev', 'tp'), split_axis=0, concat_axis=...  109 us
    all_to_all x1, blocking collectives, shards(): lax.all_to_all(partial_terms.astype(jnp.bfloat16), ('sec', 'dev', 'tp'),...  107 us
    reshape x1, local copies, waits for them, and re-layouts, shards(): flat_rows = received.reshape(device_count * slot_count, model_width)  13.7 us
    convert_element_type x1, local copies, waits for them, and re-layouts, shards(): partial_terms.astype(jnp.bfloat16)  12.8 us
    dot_general x1, matrix products, shards(): jnp.dot(hidden, down_weight, preferred_element_type=jnp.float32)  12.8 us
    convert_element_type x1, local copies, waits for them, and re-layouts, shards(): jnp.einsum('bsr,rd->bsd', placed, normed, preferred_element_type=jnp.floa...  11.4 us
    dot_general x1, matrix products, shards(): jnp.einsum('bsr,bsd->rd', placed.astype(jnp.float32), returned, precision...  7.3 us
  transfers between devices with their start and end apart: 1, of which 1 were waited for; matrix products, arithmetic and copies ran while one was open for 0% of the time, Pallas kernels for 0%

commit v1 on v0

--- a/solution.py
+++ b/solution.py
@@ -69,39 +69,22 @@
     stream = residual.astype(jnp.float32) + context.astype(jnp.float32)
     mean_square = jnp.mean(stream * stream, axis=1, keepdims=True)
     normed = (stream * lax.rsqrt(mean_square + epsilon) * norm_gain[None, :]).astype(jnp.bfloat16)
-    local_rows, model_width = normed.shape
-    device_count = lax.axis_size(("sec", "dev", "tp"))
-    top_count = active.shape[1]
-    slot_limit = max(3, (2 * local_rows * top_count + device_count - 1) // device_count)
-    targets = jnp.arange(device_count, dtype=jnp.int32)
-    naming = jnp.any(active[:, :, None] == targets[None, None, :], axis=1).astype(jnp.int32)
-    earlier = jnp.cumsum(naming, axis=0) - naming
-    slot_ids = jnp.arange(slot_limit, dtype=jnp.int32)
-    placed = (
-        (naming.T[:, None, :] == 1) & (earlier.T[:, None, :] == slot_ids[None, :, None])
-    ).astype(jnp.bfloat16)
-    outgoing = jnp.einsum("bsr,rd->bsd", placed, normed, preferred_element_type=jnp.float32).astype(
-        jnp.bfloat16
+    axes = ("sec", "dev", "tp")
+    bundle = lax.axis_index(axes)
+    named = jnp.any(active[:, :, None] == jnp.arange(128, dtype=jnp.int32)[None, None, :], axis=1)
+    packed = jnp.concatenate([normed, named.astype(jnp.bfloat16)], axis=1)
+    gathered = lax.all_gather(packed, axes, axis=0, tiled=True)
+    rows = gathered[:, :8192]
+    wanted = jnp.sum(
+        jnp.where(jnp.arange(128)[None, :] == bundle, gathered[:, 8192:].astype(jnp.float32), 0.0),
+        axis=1,
+        keepdims=True,
     )
-    received = lax.all_to_all(
-        outgoing, ("sec", "dev", "tp"), split_axis=0, concat_axis=0, tiled=True
-    )
-    slot_count = received.shape[1]
-    flat_rows = received.reshape(device_count * slot_count, model_width)
-    hidden = feed_forward(flat_rows, gate_weight, up_weight, 1.0)
-    partial_terms = jnp.dot(hidden, down_weight, preferred_element_type=jnp.float32)
-    partial_terms = partial_terms.reshape(device_count, slot_count, model_width)
-    returned = lax.all_to_all(
-        partial_terms.astype(jnp.bfloat16),
-        ("sec", "dev", "tp"),
-        split_axis=0,
-        concat_axis=0,
-        tiled=True,
-    ).astype(partial_terms.dtype)
-    update = jnp.einsum(
-        "bsr,bsd->rd", placed.astype(jnp.float32), returned, precision=lax.Precision.HIGHEST
-    )
-    return (stream + update).astype(jnp.bfloat16)
+    hidden = feed_forward(rows, gate_weight, up_weight, wanted)
+    terms = jnp.dot(hidden, down_weight, preferred_element_type=jnp.float32).astype(jnp.bfloat16)
+    terms = terms.reshape(128, 32, 1024)
+    update = lax.psum_scatter(terms, axes, scatter_dimension=0, tiled=False).reshape(4, 8192)
+    return (stream + update.astype(jnp.float32)).astype(jnp.bfloat16)
 
 
 def solution(mesh):

time: 302 us -> 1050 us (3.48)
  waiting for transfers between devices: 3.94 us -> 975 us
  blocking collectives: 216 us -> 0 us
  between operations: 0.11 us -> 13.5 us
  local copies, waits for them, and re-layouts: 38.6 us -> 27.7 us
    reduce_scatter x0 -> x1, waiting for transfers between devices: none -> 659 us  [shards(): lax.psum_scatter(terms, axes, scatter_dimension=0, tiled=False)]
    all_gather x0 -> x1, waiting for transfers between devices: none -> 312 us  [shards(): gathered = lax.all_gather(packed, axes, axis=0, tiled=True)]
    all_to_all x2 -> x0, blocking collectives: 216 us -> none  [the longest x1 109 us: shards(): lax.all_to_all(outgoing, ('sec', 'dev', 'tp'), split_axis=0, concat_axis=...]
    convert_element_type x2 -> x1, local copies, waits for them, and re-layouts: 24.2 us -> 0.94 us  [shards(): return (stream + update.astype(jnp.float32)).astype(jnp.bfloat16)]
    unnamed x10 -> x11, local copies, waits for them, and re-layouts: 0.02 us -> 12.6 us
    dot_general x3 -> x1, matrix products: 17 us -> 6.3 us  [feed_forward(): up_value = jnp.dot(row_block, up_weight, preferred_element_type=jnp.float32)]
  transfers between devices with their start and end apart: 1 -> 3, of which waited for: 1 -> 3; matrix products, arithmetic and copies ran while one was open for 0% -> 0% of each run, Pallas kernels for 0% -> 0%
where the time goes in v1:
time: 1050 us
  waiting for transfers between devices  975 us (93%)
  local copies, waits for them, and re-layouts  27.7 us (3%)
  matrix products  27.3 us (3%)
  between operations  13.5 us (1%)
    reduce_scatter x1, waiting for transfers between devices, shards(): lax.psum_scatter(terms, axes, scatter_dimension=0, tiled=False)  659 us
    all_gather x1, waiting for transfers between devices, shards(): gathered = lax.all_gather(packed, axes, axis=0, tiled=True)  312 us
  transfers between devices with their start and end apart: 3, of which 3 were waited for; matrix products, arithmetic and copies ran while one was open for 0% of the time, Pallas kernels for 0%

profile of v1, /device:TPU:0, one launch (start us, length us, event | category | flops | bytes accessed | tf_op | source)
XLA Modules:
  0.0 1051.2 jit_solution(6356441522327722411)
XLA Ops:
  6.5 0.0 copy-start
  6.5 0.0 copy-start.4
  6.5 0.9 iota_compare_fusion.1
  7.4 0.8 bitcast_convert_fusion
  8.2 1.0 fusion.41
  9.2 2.4 fusion.49
  11.6 0.0 copy-start.3
  11.6 0.2 fusion.36
  11.8 0.0 copy-start.1
  11.9 0.0 copy-start.2
  11.9 0.0 copy-done.4
  11.9 0.5 fusion.33
  12.4 0.7 convert_element_type.71
  13.0 3.3 all-to-all-start
  16.3 0.0 all-gather.3.cloned.1.call-start
  16.4 0.0 copy-done.3
  16.4 0.1 fusion.44
  16.5 3.9 all-to-all-done
  20.5 0.0 copy-done.1
  20.5 0.2 multiply_reduce_fusion
  20.7 0.0 copy-done.2
  20.7 0.1 multiply_convert_fusion
  20.8 0.6 maximum_bitcast_fusion
  21.4 0.0 all-gather.3.cloned.1.call-update
  21.4 0.0 reduce-scatter.2.cloned.1.call-start
  21.5 311.8 %all-gather.3.cloned.1.call-done = bf16[128,4,8320]{2,1,0:T(4,128)(2,1)} async-done(((bf16[1,4,8320]{2,1,0:T(4,128)(2,1)}), bf16[128,4,8320]{2,1,0:T(4,128)(2,1)}) %all-gather.3.cloned.1.call-update) | async-done | bytes 8519696 | tf_op jit(solution)/shard_map/all_gather | solution.py:76
  333.3 12.6 %reshape.81 = bf16[512,8320]{1,0:T(8,128)(2,1)} reshape(bf16[128,4,8320]{2,1,0:T(4,128)(2,1)} %all-gather.3.cloned.1.call-done) | data formatting | bytes 17039360
  345.9 1.0 select_reduce_fusion
  346.9 6.3 fusion
  353.2 0.0 copy-done
  353.2 17.2 %convolution_convert_fusion = bf16[512,8192]{1,0:T(8,128)(2,1)} fusion(bf16[128,8192]{1,0:T(8,128)(2,1)S(1)} %copy-done, f32[512,128]{1,0:T(8,128)S(1)} %fusion, bf16[8192,128]{1,0:T(8,128)(2,1)} %param.21, bf16[512,8320]{1,0:T(8,128)(2,1)} %reshape.81, f32[512]{0:T(512)S(1)} %select_reduce_fusion), kind=kOutput, calls=%fused_computation | convolution fusion | flops 2151940096 | bytes 21235712 | tf_op jit(solution)/shard_map/dot_general | solution.py:84
  370.4 13.5 %reshape.76 = bf16[128,32,1024]{2,1,0:T(8,128)(2,1)} reshape(bf16[512,8192]{1,0:T(8,128)(2,1)} %convolution_convert_fusion) | data formatting | bytes 16777216 | tf_op jit(solution)/shard_map/reshape | solution.py:85
  383.9 0.0 reduce-scatter.2.cloned.1.call-update
  383.9 658.9 %reduce-scatter.2.cloned.1.call-done = bf16[1,32,1024]{2,1,0:T(8,128)(2,1)} async-done(((bf16[128,32,1024]{2,1,0:T(8,128)(2,1)}), bf16[1,32,1024]{2,1,0:T(8,128)(2,1)}) %reduce-scatter.2.cloned.1.call-update) | async-done | bytes 65552 | tf_op jit(solution)/shard_map/reduce_scatter | solution.py:86
  1042.8 0.9 reshape.79
  1043.7 0.7 add_convert_fusion
  (7 shorter events, 0.1 us)
Async XLA Ops:
  6.5 346.7 %copy-start = (bf16[128,8192]{1,0:T(8,128)(2,1)S(1)}, bf16[128,8192]{1,0:T(8,128)(2,1)}, u32[]{:S(2)}) copy-start(bf16[128,8192]{1,0:T(8,128)(2,1)} %param.23) | copy-start | bytes 6291460
  6.5 5.4 copy-start.4
  11.6 4.8 copy-start.3
  11.8 8.6 copy-start.1
  11.9 8.8 copy-start.2
  13.0 7.4 all-to-all-start
  16.3 317.0 %all-gather.3.cloned.1.call-start = ((), (), s32[]{:S(2)}) async-start(), calls=%async_computation.3 | async-start | bytes 8586240 | tf_op jit(solution)/shard_map/all_gather | solution.py:76
  21.4 1021.3 %reduce-scatter.2.cloned.1.call-start = ((), (), s32[]{:S(2)}) async-start(), calls=%async_computation.2 | async-start | bytes 8454144 | tf_op jit(solution)/shard_map/reduce_scatter | solution.py:86
Sparse Core Ops, SparseCore 0:
  21.6 311.6 all-gather.2
  384.0 658.6 reduce-scatter.1

commit v2 on v1

v2 whole, which is shorter than its diff:
```python
import functools

import jax
import jax.numpy as jnp
from jax import lax
from jax.experimental import pallas as pl
from jax.experimental.pallas import tpu as pltpu
from jax.sharding import PartitionSpec as P

MESH = pl.DeviceIdType.MESH
EPSILON = 1e-05
F32 = jnp.float32
BF16 = jnp.bfloat16

ROWS = 8
HALF = 4096
WIDTH = HALF + 128
SPANS = ((0, 1408), (1408, 2816), (2816, 4224))
TERMS = ((0, 1408), (1408, 2816), (2816, 4096))
ORDERS = (("x", "y", "z"), ("y", "z", "x"), ("z", "x", "y"))
COPIES = 256


def cut(lo, hi):
    middle = lo + ((hi - lo) // 128 + 1) // 2 * 128
    return (lo, middle), (middle, hi)


def kernel(
    lengths, queries, new_keys, token_values, residual, gain, active,
    key_cache, stored_values, gate, up, down,
    out,
    keys, values, w, d, g, acc, hid, stream, scores, probs, blend, other_resid, to_tp, from_tp,
    send_two, send_plus, send_minus, got_two_plus, got_two_minus, got_plus, got_minus, total,
    line_two, line_plus, line_minus, line_got_two_plus, line_got_two_minus, line_got_plus, line_got_minus,
    unit_two, unit_plus, unit_minus, unit_got_two, unit_got_plus, unit_got_minus,
    send_sems, recv_sems, local_sems,
):
    sec, dev, tp = lax.axis_index("sec"), lax.axis_index("dev"), lax.axis_index("tp")
    core = lax.rem(dev, 2)
    here = {"x": lax.rem(dev // 2, 4), "y": sec * 2 + tp, "z": dev // 8}

    def device(x, y, z, core):
        return (y // 2, (z * 4 + x) * 2 + core, lax.rem(y, 2))

    def along(dim, step):
        at = dict(here)
        at[dim] = lax.rem(here[dim] + step + 4, 4)
        return device(at["x"], at["y"], at["z"], core)

    twin = device(here["x"], here["y"], here["z"], 1 - core)
    pair = (sec, dev, 1 - tp)

    started = []

    def send(src, dst, target):
        i = len(started)
        copy = pltpu.make_async_remote_copy(
            src_ref=src, dst_ref=dst, send_sem=send_sems.at[i], recv_sem=recv_sems.at[i],
            device_id=target, device_id_type=MESH,
        )
        copy.start()
        started.append(copy)
        return i

    def arrive(i, dst):
        pltpu.make_async_remote_copy(
            src_ref=dst, dst_ref=dst, send_sem=send_sems.at[i], recv_sem=recv_sems.at[i],
            device_id=twin, device_id_type=MESH,
        ).wait_recv()

    local = []

    def fetch(src, dst):
        copy = pltpu.make_async_copy(src, dst, local_sems.at[len(local)])
        copy.start()
        local.append(copy)
        return copy

    key_rows = [fetch(key_cache.at[r], keys.at[r]) for r in range(ROWS)]
    value_rows = [fetch(stored_values.at[r], values.at[r]) for r in range(ROWS)]
    mine = pl.ds(pl.multiple_of(core * 128, 128), 128)
    mine_up = pl.ds(pl.multiple_of(256 + core * 128, 128), 128)
    pieces = []
    for t in range(2):
        rows = slice(t * HALF, (t + 1) * HALF)
        pieces.append((gate.at[rows, :], w.at[t, :, mine]))
        pieces.append((up.at[rows, :], w.at[t, :, mine_up]))
    for t in range(2):
        pieces.append((down.at[:, slice(t * HALF, (t + 1) * HALF)], d.at[t, mine, :]))
    weights = [fetch(src, dst) for src, dst in pieces]

    barrier = pltpu.get_barrier_semaphore()
    greeted = [twin] + [along(dim, step) for dim in ("x", "y", "z") for step in (1, -1)]
    for target in greeted:
        pl.semaphore_signal(barrier, inc=1, device_id=target, device_id_type=MESH)
    pl.semaphore_wait(barrier, len(greeted))

    theirs_half = pl.ds(pl.multiple_of((1 - tp) * HALF, 128), HALF)
    resid_id = send(residual.at[:, theirs_half], other_resid, pair)
    weight_ids = [send(src, dst, twin) for src, dst in pieces]

    first = tp == 0
    scale = 128 ** (-0.5)
    row_of = lax.rem(lax.broadcasted_iota(jnp.int32, (64, 1), 0), ROWS)
    limit = jnp.zeros((64, 1), jnp.int32)
    for r in range(ROWS):
        limit = jnp.where(row_of == r, lengths[r], limit)
    grouped = []
    for j in range(4):
        grouped.append(jnp.concatenate(
            [queries[:, (j * 8 + i) * 128:(j * 8 + i + 1) * 128].astype(F32) for i in range(8)], axis=0))
    for r in range(ROWS):
        key_rows[r].wait()
        for j in range(4):
            s = lax.dot_general(
                grouped[j].astype(BF16), keys[r, :, j * 128:(j + 1) * 128], (((1,), (1,)), ((), ())),
                preferred_element_type=F32)
            scores[j] = s if r == 0 else jnp.where(row_of == r, s, scores[j])
    column = lax.broadcasted_iota(jnp.int32, (64, 256), 1)
    fresh_probs = []
    for j in range(4):
        s = jnp.where(column < limit, scores[j] * scale, -1e30)
        fresh_key = jnp.concatenate([new_keys[:, j * 128:(j + 1) * 128].astype(F32)] * 8, axis=0)
        fresh = jnp.sum(grouped[j] * fresh_key, axis=1, keepdims=True) * scale
        highest = jnp.maximum(jnp.max(s, axis=1, keepdims=True), fresh)
        e = jnp.exp(s - highest)
        fresh_e = jnp.exp(fresh - highest)
        denominator = jnp.sum(e, axis=1, keepdims=True) + fresh_e
        probs[j] = (e / denominator).astype(BF16)
        fresh_probs.append((fresh_e / denominator).astype(BF16).astype(F32))
    for r in range(ROWS):
        value_rows[r].wait()
        for j in range(4):
            o = jnp.dot(probs[j], values[r, :, j * 128:(j + 1) * 128], preferred_element_type=F32)
            blend[j] = o if r == 0 else jnp.where(row_of == r, o, blend[j])

    lane = lax.broadcasted_iota(jnp.int32, (4, 128), 1)
    named = jnp.zeros((4, 128), F32)
    for k in range(16):
        named = jnp.where(active[:, k:k + 1] == lane, 1.0, named)

    arrive(resid_id, other_resid)
    me = (here["y"], here["z"], here["x"])
    squares = jnp.zeros((ROWS, 128), F32)
    for j in range(4):
        fresh_value = jnp.concatenate([token_values[:, j * 128:(j + 1) * 128].astype(F32)] * 8, axis=0)
        block = (blend[j] + fresh_probs[j] * fresh_value).astype(BF16).astype(F32)
        for i in range(8):
            lo = (j * 8 + i) * 128
            own = jnp.where(first, residual[:, lo:lo + 128], residual[:, HALF + lo:HALF + lo + 128]).astype(F32)
            other = other_resid[:, lo:lo + 128].astype(F32)
            resid = jnp.concatenate(
                [jnp.where(first, own, other), jnp.where(first, other, own)], axis=0)
            value = resid + block[i * 8:(i + 1) * 8]
            stream[:, lo:lo + 128] = value
            squares = squares + value * value
            factor = jnp.where(first, gain[:, lo:lo + 128], gain[:, HALF + lo:HALF + lo + 128])
            g[me + (slice(None), slice(lo, lo + 128))] = (value * factor).astype(BF16)
    sub8 = lax.broadcasted_iota(jnp.int32, (ROWS, 128), 0)
    lane8 = lax.broadcasted_iota(jnp.int32, (ROWS, 128), 1)
    row_sums = jnp.sum(squares, axis=1, keepdims=True)
    sums = jnp.sum(jnp.where(sub8 == lane8, row_sums, 0.0), axis=0, keepdims=True)
    sums_hi = sums.astype(BF16).astype(F32)
    sums_lo = sums - sums_hi
    lower = lax.broadcasted_iota(jnp.int32, (4, 128), 0)
    told = jnp.where(lower == 0, sums_hi, jnp.where(lower == 1, sums_lo, 0.0))
    extra = jnp.concatenate([jnp.where(first, named, told), jnp.where(first, told, named)], axis=0)
    g[me + (slice(None), slice(HALF, WIDTH))] = extra.astype(BF16)

    def spot(at, columns):
        index = tuple(at[dim] if dim in at else slice(None) for dim in ("y", "z", "x"))
        return g.at[index + (slice(None), slice(*columns))]

    def near(dim, step):
        return lax.rem(here[dim] + step + 4, 4)

    class Ring:
        def __init__(self, k, dim, fixed):
            self.columns, self.dim, self.fixed = SPANS[k], dim, fixed

        def region(self, step, columns):
            at = dict(self.fixed)
            at[self.dim] = near(self.dim, step)
            return spot(at, columns)

        def open(self):
            part = self.region(0, self.columns)
            self.plus = send(part, part, along(self.dim, 1))
            self.minus = send(part, part, along(self.dim, -1))

        def relay(self):
            one, two = cut(*self.columns)
            arrive(self.plus, self.region(-1, self.columns))
            part = self.region(-1, one)
            self.far_one = send(part, part, along(self.dim, 1))
            arrive(self.minus, self.region(1, self.columns))
            part = self.region(1, two)
            self.far_two = send(part, part, along(self.dim, -1))

        def close(self):
            one, two = cut(*self.columns)
            arrive(self.far_one, self.region(2, one))
            arrive(self.far_two, self.region(2, two))

    parts = range(3)
    rings = []
    for k in parts:
        a, b, c = ORDERS[k]
        units = Ring(k, a, {b: here[b], c: here[c]})
        lines = Ring(k, b, {c: here[c]})
        slabs = {step: Ring(k, c, {b: near(b, step)}) for step in (0, -1, 1, 2)}
        rings.append((units, lines, slabs))

    def multiply(k, step):
        lo, hi = SPANS[k][0], min(SPANS[k][1], HALF)
        c = ORDERS[k][2]
        at = near(c, step)
        columns = slice(lo, hi)
        n = hi - lo
        if c == "y":
            rows = g[at, :, :, :, columns].reshape(128, n)
            part = jnp.dot(rows, w[lax.rem(at, 2), columns, :], preferred_element_type=F32)
            acc[at // 2] += part.reshape(4, 4, ROWS, 512)
            return
        part = 0.0
        for t in range(2):
            if c == "z":
                rows = jnp.concatenate([g[y, at, :, :, columns].reshape(32, n) for y in (t, 2 + t)], axis=0)
            else:
                rows = jnp.concatenate([g[y, :, at, :, columns].reshape(32, n) for y in (t, 2 + t)], axis=0)
            part = part + jnp.dot(rows, w[t, columns, :], preferred_element_type=F32)
        part = part.reshape(2, 4, ROWS, 512)
        if c == "z":
            acc[:, at] += part
        else:
            acc[:, :, at] += part

    for k in parts:
        rings[k][0].open()
    acc[...] = jnp.zeros_like(acc)
    for k in parts:
        rings[k][0].relay()
    for k in parts:
        rings[k][0].close()
        rings[k][1].open()
        rings[k][2][0].open()
    for k in parts:
        rings[k][1].relay()
        rings[k][2][-1].open()
        rings[k][2][1].open()
    for k in parts:
        rings[k][2][0].relay()
    for k in parts:
        rings[k][1].close()
        rings[k][2][2].open()
    for copy in weights[:4]:
        copy.wait()
    for i in range(4):
        arrive(weight_ids[i], w.at[i // 2, :, pl.ds(pl.multiple_of((1 - core) * 128 + i % 2 * 256, 128), 128)])
    for k in parts:
        multiply(k, 0)
    for step in (-1, 1, 2):
        for k in parts:
            rings[k][2][step].relay()
    for k in parts:
        multiply(k, -1)
        multiply(k, 1)
    for k in parts:
        for step in (0, -1, 1, 2):
            rings[k][2][step].close()
        multiply(k, 2)

    sub = lax.broadcasted_iota(jnp.int32, (32, ROWS, 128), 1)
    lanes = lax.broadcasted_iota(jnp.int32, (32, ROWS, 128), 2)
    extras = []
    for t in range(2):
        extras.append(jnp.concatenate(
            [g[y, :, :, :, HALF:WIDTH].astype(F32).reshape(16, ROWS, 128) for y in (t, 2 + t)], axis=0))
    names = jnp.where(sub < 4, extras[0], extras[1])
    bundle = sec * 64 + (dev - core) * 2 + tp
    wanted = [
        jnp.sum(jnp.where(lanes == bundle + 2 * i, names, 0.0), axis=2, keepdims=True).reshape(256, 1)
        for i in range(2)
    ]
    sums = (extras[0][:, 4:5] + extras[0][:, 5:6]) + (extras[1][:, 0:1] + extras[1][:, 1:2])
    mean = jnp.sum(jnp.where(lanes == sub, sums, 0.0), axis=2, keepdims=True).reshape(256, 1) / 8192.0
    inverse = lax.rsqrt(mean + EPSILON)
    gate_value = acc[:, :, :, :, 0:256].reshape(256, 256) * inverse
    up_value = acc[:, :, :, :, 256:512].reshape(256, 256) * inverse
    low = lax.broadcasted_iota(jnp.int32, (256, 256), 1) < 128
    hidden = jnp.maximum(gate_value, 0.0) * up_value * jnp.where(low, wanted[0], wanted[1])
    hid[...] = hidden.astype(BF16).reshape(2, 4, 4, ROWS, 256)

    for copy in weights[4:]:
        copy.wait()
    for i in range(2):
        arrive(weight_ids[4 + i], d.at[i, pl.ds(pl.multiple_of((1 - core) * 128, 128), 128), :])

    def terms(k, step, store):
        c = ORDERS[k][2]
        at = near(c, step)
        columns = slice(*TERMS[k])
        n = TERMS[k][1] - TERMS[k][0]
        if c == "y":
            rows = hid[at // 2].reshape(128, 256)
            part = jnp.dot(rows, d[lax.rem(at, 2), :, columns], preferred_element_type=F32)
            store(slice(None), part.reshape(4, 4, ROWS, n))
            return
        rows = (hid[:, at] if c == "z" else hid[:, :, at]).reshape(64, 256)
        for t in range(2):
            part = jnp.dot(rows, d[t, :, columns], preferred_element_type=F32).reshape(2, 4, ROWS, n)
            store(t, part[0])
            store(2 + t, part[1])

    def width(k):
        return TERMS[k][1] - TERMS[k][0]

    def line(ref, k, step, columns=None):
        a, b, c = ORDERS[k]
        at = near(b, step)
        columns = slice(0, width(k)) if columns is None else slice(*columns)
        lead = (at,) if b == "y" else (slice(None), at)
        rest = (slice(None),) if b == "y" else ()
        return ref.at[(k,) + lead + rest + (slice(None), columns)]

    def fill(ref, k):
        def store(y, value):
            if isinstance(y, slice):
                ref[k, :, :, :, 0:width(k)] = value.astype(ref.dtype)
            else:
                ref[k, y, :, :, 0:width(k)] = value.astype(ref.dtype)
        return store

    order = (2, 1, -1, 0)
    ids = {}
    for k in parts:
        c = ORDERS[k][2]
        one, two = cut(0, width(k))
        terms(k, 2, fill(send_two, k))
        for step in order:
            ids[k, step, "two_plus"] = send(line(send_two, k, step, one), line(got_two_plus, k, step, one), along(c, 1))
            ids[k, step, "two_minus"] = send(line(send_two, k, step, two), line(got_two_minus, k, step, two), along(c, -1))
    for k in parts:
        c = ORDERS[k][2]
        one, two = cut(0, width(k))
        terms(k, 1, fill(send_plus, k))
        terms(k, -1, fill(send_minus, k))
        for step in order:
            ids[k, step, "plus_two"] = send(line(send_plus, k, step, two), line(got_plus, k, step, two), along(c, 1))
            ids[k, step, "minus_one"] = send(line(send_minus, k, step, one), line(got_minus, k, step, one), along(c, -1))
    for k in parts:
        terms(k, 0, fill(total, k))

    def add_into(ref, *others):
        value = ref[...].astype(F32)
        for other in others:
            value = value + other[...].astype(F32)
        ref[...] = value.astype(ref.dtype)

    for step in order:
        for k in parts:
            c = ORDERS[k][2]
            one, two = cut(0, width(k))
            arrive(ids[k, step, "two_plus"], line(got_two_plus, k, step, one))
            add_into(line(send_plus, k, step, one), line(got_two_plus, k, step, one))
            ids[k, step, "plus_one"] = send(line(send_plus, k, step, one), line(got_plus, k, step, one), along(c, 1))
            arrive(ids[k, step, "two_minus"], line(got_two_minus, k, step, two))
            add_into(line(send_minus, k, step, two), line(got_two_minus, k, step, two))
            ids[k, step, "minus_two"] = send(line(send_minus, k, step, two), line(got_minus, k, step, two), along(c, -1))

    for step in order:
        for k in parts:
            b = ORDERS[k][1]
            n = width(k)
            one, two = cut(0, n)
            one_s, two_s, all_s = slice(*one), slice(*two), slice(0, n)
            arrive(ids[k, step, "plus_two"], line(got_plus, k, step, two))
            arrive(ids[k, step, "plus_one"], line(got_plus, k, step, one))
            arrive(ids[k, step, "minus_one"], line(got_minus, k, step, one))
            arrive(ids[k, step, "minus_two"], line(got_minus, k, step, two))
            value = (line(total, k, step)[...] + line(got_plus, k, step)[...].astype(F32)
                     + line(got_minus, k, step)[...].astype(F32))
            if step == 2:
                line_two[k, :, :, all_s] = value.astype(BF16)
                ids[k, "two_plus"] = send(
                    line_two.at[k, :, :, one_s], line_got_two_plus.at[k, :, :, one_s], along(b, 1))
                ids[k, "two_minus"] = send(
                    line_two.at[k, :, :, two_s], line_got_two_minus.at[k, :, :, two_s], along(b, -1))
            elif step == 1:
                line_plus[k, :, :, all_s] = value.astype(BF16)
                ids[k, "plus_two"] = send(
                    line_plus.at[k, :, :, two_s], line_got_plus.at[k, :, :, two_s], along(b, 1))
            elif step == -1:
                line_minus[k, :, :, all_s] = value.astype(BF16)
                ids[k, "minus_one"] = send(
                    line_minus.at[k, :, :, one_s], line_got_minus.at[k, :, :, one_s], along(b, -1))
            else:
                line(total, k, 0)[...] = value
            if step == -1:
                arrive(ids[k, "two_plus"], line_got_two_plus.at[k, :, :, one_s])
                add_into(line_plus.at[k, :, :, one_s], line_got_two_plus.at[k, :, :, one_s])
                ids[k, "plus_one"] = send(
                    line_plus.at[k, :, :, one_s], line_got_plus.at[k, :, :, one_s], along(b, 1))
                arrive(ids[k, "two_minus"], line_got_two_minus.at[k, :, :, two_s])
                add_into(line_minus.at[k, :, :, two_s], line_got_two_minus.at[k, :, :, two_s])
                ids[k, "minus_two"] = send(
                    line_minus.at[k, :, :, two_s], line_got_minus.at[k, :, :, two_s], along(b, -1))

    for k in parts:
        a = ORDERS[k][0]
        n = width(k)
        one, two = cut(0, n)
        one_s, two_s, all_s = slice(*one), slice(*two), slice(0, n)
        arrive(ids[k, "plus_two"], line_got_plus.at[k, :, :, two_s])
        arrive(ids[k, "plus_one"], line_got_plus.at[k, :, :, one_s])
        arrive(ids[k, "minus_one"], line_got_minus.at[k, :, :, one_s])
        arrive(ids[k, "minus_two"], line_got_minus.at[k, :, :, two_s])
        add_into(line(total, k, 0), line_got_plus.at[k, :, :, all_s], line_got_minus.at[k, :, :, all_s])
        whole = line(total, k, 0)
        unit_two[k, :, all_s] = whole.at[near(a, 2)][...].astype(BF16)
        ids[k, "unit_two"] = send(unit_two.at[k, :, all_s], unit_got_two.at[k, :, all_s], along(a, 1))
        unit_minus[k, :, all_s] = whole.at[near(a, -1)][...].astype(BF16)
        ids[k, "unit_minus"] = send(unit_minus.at[k, :, all_s], unit_got_minus.at[k, :, all_s], along(a, -1))
    for k in parts:
        a = ORDERS[k][0]
        all_s = slice(0, width(k))
        arrive(ids[k, "unit_two"], unit_got_two.at[k, :, all_s])
        value = line(total, k, 0).at[near(a, 1)][...] + unit_got_two[k, :, all_s].astype(F32)
        unit_plus[k, :, all_s] = value.astype(BF16)
        ids[k, "unit_plus"] = send(unit_plus.at[k, :, all_s], unit_got_plus.at[k, :, all_s], along(a, 1))
    kept = []
    for k in parts:
        a = ORDERS[k][0]
        all_s = slice(0, width(k))
        arrive(ids[k, "unit_minus"], unit_got_minus.at[k, :, all_s])
        arrive(ids[k, "unit_plus"], unit_got_plus.at[k, :, all_s])
        value = (line(total, k, 0).at[near(a, 0)][...] + unit_got_plus[k, :, all_s].astype(F32)
                 + unit_got_minus[k, :, all_s].astype(F32))
        value = stream[:, slice(*TERMS[k])] + value
        kept.append(jnp.where(first, value[0:4], value[4:8]).astype(BF16))
        to_tp[:, slice(*TERMS[k])] = jnp.where(first, value[4:8], value[0:4]).astype(BF16)
    last = send(to_tp, from_tp, pair)
    arrive(last, from_tp)
    for k in parts:
        lo, hi = TERMS[k]
        theirs = from_tp[:, lo:hi]
        out[:, lo:hi] = jnp.where(first, kept[k], theirs)
        out[:, HALF + lo:HALF + hi] = jnp.where(first, theirs, kept[k])
    for copy in started:
        copy.wait_send()


def shards(
    queries, new_keys, token_values, key_cache, stored_values, cache_lengths, residual, norm_gain,
    active, gate_weight, up_weight, down_weight,
):
    vmem = pl.BlockSpec(memory_space=pltpu.VMEM)
    hbm = pl.BlockSpec(memory_space=pl.ANY)
    slab = (3, 4, 4, ROWS, 1408)
    rows = (3, 4, ROWS, 1408)
    unit = (3, ROWS, 1408)
    return pl.pallas_call(
        kernel,
        out_shape=jax.ShapeDtypeStruct((4, 8192), BF16),
        in_specs=[pl.BlockSpec(memory_space=pltpu.SMEM)] + [vmem] * 6 + [hbm] * 5,
        out_specs=vmem,
        scratch_shapes=[
            pltpu.VMEM((ROWS, 256, 512), BF16),
            pltpu.VMEM((ROWS, 256, 512), BF16),
            pltpu.VMEM((2, HALF, 512), BF16),
            pltpu.VMEM((2, 256, HALF), BF16),
            pltpu.VMEM((4, 4, 4, ROWS, WIDTH), BF16),
            pltpu.VMEM((2, 4, 4, ROWS, 512), F32),
            pltpu.VMEM((2, 4, 4, ROWS, 256), BF16),
            pltpu.VMEM((ROWS, HALF), F32),
            pltpu.VMEM((4, 64, 256), F32),
            pltpu.VMEM((4, 64, 256), BF16),
            pltpu.VMEM((4, 64, 128), F32),
            pltpu.VMEM((4, HALF), BF16),
            pltpu.VMEM((4, HALF), BF16),
            pltpu.VMEM((4, HALF), BF16),
        ]
        + [pltpu.VMEM(slab, BF16)] * 7
        + [pltpu.VMEM(slab, F32)]
        + [pltpu.VMEM(rows, BF16)] * 7
        + [pltpu.VMEM(unit, BF16)] * 6
        + [
            pltpu.SemaphoreType.DMA((COPIES,)),
            pltpu.SemaphoreType.DMA((COPIES,)),
            pltpu.SemaphoreType.DMA((32,)),
        ],
        compiler_params=pltpu.CompilerParams(
            collective_id=0, has_side_effects=True, vmem_limit_bytes=60 * 2**20),
    )(cache_lengths, queries, new_keys, token_values, residual, norm_gain.reshape(1, 8192), active,
      key_cache, stored_values, gate_weight, up_weight, down_weight)


def solution(mesh):
    return jax.shard_map(
        shards,
        mesh=mesh,
        in_specs=(
            P(("sec", "dev"), "tp"),
            P(("sec", "dev"), "tp"),
            P(("sec", "dev"), "tp"),
            P(("sec", "dev"), None, "tp"),
            P(("sec", "dev"), None, "tp"),
            P(("sec", "dev")),
            P(("sec", "dev", "tp"), None),
            P(),
            P(("sec", "dev", "tp"), None),
            P(None, ("sec", "dev", "tp")),
            P(None, ("sec", "dev", "tp")),
            P(("sec", "dev", "tp"), None),
        ),
        out_specs=P(("sec", "dev", "tp"), None),
        check_vma=False,
    )
```

time: 1050 us -> 75.4 us (0.07)
  waiting for transfers between devices: 975 us -> 0 us
  Pallas kernels: 0 us -> 73 us
  matrix products: 27.3 us -> 0 us
  local copies, waits for them, and re-layouts: 27.7 us -> 1.49 us
  between operations: 13.5 us -> 0.01 us
    reduce_scatter x1 -> x0, waiting for transfers between devices: 659 us -> none  [shards(): lax.psum_scatter(terms, axes, scatter_dimension=0, tiled=False)]
    all_gather x1 -> x0, waiting for transfers between devices: 312 us -> none  [shards(): gathered = lax.all_gather(packed, axes, axis=0, tiled=True)]
    pallas_call x0 -> x1, Pallas kernels: none -> 73 us  [shards(): pl.pallas_call(kernel, out_shape=jax.ShapeDtypeStruct((4, 8192), BF16), i...]
    dot_general x5 -> x0, matrix products: 27.3 us -> none  [the longest x1 17.2 us: shards(): jnp.dot(hidden, down_weight, preferred_element_type=jnp.float32)]
    reshape x1 -> x0, local copies, waits for them, and re-layouts: 13.5 us -> none  [shards(): terms = terms.reshape(128, 32, 1024)]
    unnamed x11 -> x1, local copies, waits for them, and re-layouts: 12.6 us -> 1.49 us
  transfers between devices with their start and end apart: 3 -> 0, of which waited for: 3 -> 0; matrix products, arithmetic and copies ran while one was open for 0% -> 0% of each run, Pallas kernels for 0% -> 0%
where the time goes in v2:
time: 75.4 us; the launch traced here: 74.5 us
  Pallas kernels  73 us (97%)
  local copies, waits for them, and re-layouts  1.49 us (2%)
    pallas_call x1, Pallas kernels, shards(): pl.pallas_call(kernel, out_shape=jax.ShapeDtypeStruct((4, 8192), BF16), i...  73 us

profile of v2, /device:TPU:0, one launch (start us, length us, event | category | flops | bytes accessed | tf_op | source)
XLA Modules:
  0.0 74.5 jit_solution(16304564859245231394)
XLA Ops:
  0.0 73.0 %shard_map.118 = bf16[4,8192]{1,0:T(4,128)(2,1)} custom-call(s32[8]{0:T(128)} %lengths.1, bf16[8,4096]{1,0:T(8,128)(2,1)} %queries.1, bf16[8,512]{1,0:T(8,128)(2,1)} %new_keys.1, bf16[8,512]{1,0:T(8,128)(2,1)} %token_values.1, bf16[4,8192]{1,0:T(4,128)(2,1)} %residual.1, f32[1,8192]{1,0:T(1,128)} %bitcast.1, s32[4,16]{1,0:T(4,128)} %active.1, ...), custom_call_target="tpu_custom_call" | custom-call | tf_op jit(solution)/shard_map/pallas_call | solution.py:463
  73.0 1.5 %copy.14 = bf16[4,8192]{1,0:T(4,128)(2,1)} copy(bf16[4,8192]{1,0:T(4,128)(2,1)} %shard_map.118) | data formatting | bytes 131072

commit v3 on v2

--- a/solution.py
+++ b/solution.py
@@ -18,7 +18,9 @@
 SPANS = ((0, 1408), (1408, 2816), (2816, 4224))
 TERMS = ((0, 1408), (1408, 2816), (2816, 4096))
 ORDERS = (("x", "y", "z"), ("y", "z", "x"), ("z", "x", "y"))
-COPIES = 256
+SENDS = 10
+ARRIVALS = 128
+FETCHES = 18
 
 
 def cut(lo, hi):
@@ -51,34 +53,37 @@
     twin = device(here["x"], here["y"], here["z"], 1 - core)
     pair = (sec, dev, 1 - tp)
 
-    started = []
-
-    def send(src, dst, target):
-        i = len(started)
-        copy = pltpu.make_async_remote_copy(
-            src_ref=src, dst_ref=dst, send_sem=send_sems.at[i], recv_sem=recv_sems.at[i],
+    used = []
+
+    def arrival():
+        used.append(None)
+        return len(used) - 1
+
+    def send(group, i, src, dst, target):
+        pltpu.make_async_remote_copy(
+            src_ref=src, dst_ref=dst, send_sem=send_sems.at[group], recv_sem=recv_sems.at[i],
             device_id=target, device_id_type=MESH,
-        )
-        copy.start()
-        started.append(copy)
-        return i
+        ).start()
 
     def arrive(i, dst):
         pltpu.make_async_remote_copy(
-            src_ref=dst, dst_ref=dst, send_sem=send_sems.at[i], recv_sem=recv_sems.at[i],
+            src_ref=dst, dst_ref=dst, send_sem=send_sems.at[0], recv_sem=recv_sems.at[i],
             device_id=twin, device_id_type=MESH,
         ).wait_recv()
 
-    local = []
-
-    def fetch(src, dst):
-        copy = pltpu.make_async_copy(src, dst, local_sems.at[len(local)])
+    def sent(group, src):
+        pltpu.make_async_remote_copy(
+            src_ref=src, dst_ref=src, send_sem=send_sems.at[group], recv_sem=recv_sems.at[0],
+            device_id=twin, device_id_type=MESH,
+        ).wait_send()
+
+    def fetch(src, dst, i):
+        copy = pltpu.make_async_copy(src, dst, local_sems.at[i])
         copy.start()
-        local.append(copy)
         return copy
 
-    key_rows = [fetch(key_cache.at[r], keys.at[r]) for r in range(ROWS)]
-    value_rows = [fetch(stored_values.at[r], values.at[r]) for r in range(ROWS)]
+    key_rows = [fetch(key_cache.at[r], keys.at[r], r) for r in range(ROWS)]
+    value_rows = [fetch(stored_values.at[r], values.at[r], ROWS + r) for r in range(ROWS)]
     mine = pl.ds(pl.multiple_of(core * 128, 128), 128)
     mine_up = pl.ds(pl.multiple_of(256 + core * 128, 128), 128)
     pieces = []
@@ -88,7 +93,9 @@
         pieces.append((up.at[rows, :], w.at[t, :, mine_up]))
     for t in range(2):
         pieces.append((down.at[:, slice(t * HALF, (t + 1) * HALF)], d.at[t, mine, :]))
-    weights = [fetch(src, dst) for src, dst in pieces]
+    for n, (src, dst) in enumerate(pieces):
+        fetch(src, dst, 16 + n // 4)
+    w_bytes, d_bytes = w.at[:, :, 0:256], d.at[:, 0:128, :]
 
     barrier = pltpu.get_barrier_semaphore()
     greeted = [twin] + [along(dim, step) for dim in ("x", "y", "z") for step in (1, -1)]
@@ -97,8 +104,10 @@
     pl.semaphore_wait(barrier, len(greeted))
 
     theirs_half = pl.ds(pl.multiple_of((1 - tp) * HALF, 128), HALF)
-    resid_id = send(residual.at[:, theirs_half], other_resid, pair)
-    weight_ids = [send(src, dst, twin) for src, dst in pieces]
+    resid_id, w_id, d_id = arrival(), arrival(), arrival()
+    send(0, resid_id, residual.at[:, theirs_half], other_resid, pair)
+    for n, (src, dst) in enumerate(pieces):
+        send(1 + n // 4, (w_id, d_id)[n // 4], src, dst, twin)
 
     first = tp == 0
     scale = 128 ** (-0.5)
@@ -176,8 +185,8 @@
         return lax.rem(here[dim] + step + 4, 4)
 
     class Ring:
-        def __init__(self, k, dim, fixed):
-            self.columns, self.dim, self.fixed = SPANS[k], dim, fixed
+        def __init__(self, k, group, dim, fixed, far):
+            self.columns, self.group, self.dim, self.fixed, self.far = SPANS[k], group, dim, fixed, far
 
         def region(self, step, columns):
             at = dict(self.fixed)
@@ -186,31 +195,36 @@
 
         def open(self):
             part = self.region(0, self.columns)
-            self.plus = send(part, part, along(self.dim, 1))
-            self.minus = send(part, part, along(self.dim, -1))
+            self.plus, self.minus = arrival(), arrival()
+            send(self.group, self.plus, part, part, along(self.dim, 1))
+            send(self.group, self.minus, part, part, along(self.dim, -1))
 
         def relay(self):
             one, two = cut(*self.columns)
             arrive(self.plus, self.region(-1, self.columns))
             part = self.region(-1, one)
-            self.far_one = send(part, part, along(self.dim, 1))
+            send(self.group, self.far, part, part, along(self.dim, 1))
             arrive(self.minus, self.region(1, self.columns))
             part = self.region(1, two)
-            self.far_two = send(part, part, along(self.dim, -1))
-
-        def close(self):
-            one, two = cut(*self.columns)
-            arrive(self.far_one, self.region(2, one))
-            arrive(self.far_two, self.region(2, two))
+            send(self.group, self.far, part, part, along(self.dim, -1))
 
     parts = range(3)
+    around = (0, 1, -1, 2)
     rings = []
     for k in parts:
         a, b, c = ORDERS[k]
-        units = Ring(k, a, {b: here[b], c: here[c]})
-        lines = Ring(k, b, {c: here[c]})
-        slabs = {step: Ring(k, c, {b: near(b, step)}) for step in (0, -1, 1, 2)}
-        rings.append((units, lines, slabs))
+        far = [arrival() for _ in range(3)]
+        units = Ring(k, 3, a, {b: here[b], c: here[c]}, far[0])
+        second = {step: Ring(k, 4, b, {a: near(a, step), c: here[c]}, far[1]) for step in around}
+        third = {step: Ring(k, 5, c, {a: near(a, step), b: here[b]}, far[2]) for step in around}
+        lines = {step: Ring(k, 5, c, {b: near(b, step)}, far[2]) for step in (1, -1, 2)}
+        rings.append((units, second, third, lines))
+
+    def close(k, phase):
+        dims = ORDERS[k][:phase + 1]
+        at = {dim: here[dim] for dim in ORDERS[k][phase + 1:]}
+        at[dims[-1]] = near(dims[-1], 2)
+        arrive(rings[k][phase].far if phase == 0 else rings[k][phase][0].far, spot(at, SPANS[k]))
 
     def multiply(k, step):
         lo, hi = SPANS[k][0], min(SPANS[k][1], HALF)
@@ -236,39 +250,52 @@
         else:
             acc[:, :, at] += part
 
-    for k in parts:
-        rings[k][0].open()
+    for phase in range(3):
+        for k in parts:
+            (rings[k][0] if phase == 0 else rings[k][phase][0]).open()
     acc[...] = jnp.zeros_like(acc)
     for k in parts:
         rings[k][0].relay()
-    for k in parts:
-        rings[k][0].close()
-        rings[k][1].open()
-        rings[k][2][0].open()
-    for k in parts:
-        rings[k][1].relay()
-        rings[k][2][-1].open()
-        rings[k][2][1].open()
+    for phase in (1, 2):
+        for k in parts:
+            rings[k][phase][1].open()
+            rings[k][phase][-1].open()
+    for k in parts:
+        rings[k][1][0].relay()
+    for k in parts:
+        close(k, 0)
+        rings[k][1][2].open()
+    for k in parts:
+        rings[k][2][2].open()
     for k in parts:
         rings[k][2][0].relay()
     for k in parts:
-        rings[k][1].close()
-        rings[k][2][2].open()
-    for copy in weights[:4]:
-        copy.wait()
-    for i in range(4):
-        arrive(weight_ids[i], w.at[i // 2, :, pl.ds(pl.multiple_of((1 - core) * 128 + i % 2 * 256, 128), 128)])
+        rings[k][1][1].relay()
+        rings[k][1][-1].relay()
+    for k in parts:
+        rings[k][1][2].relay()
+    for k in parts:
+        rings[k][3][1].open()
+        rings[k][3][-1].open()
+    for k in parts:
+        rings[k][2][1].relay()
+        rings[k][2][-1].relay()
+    for k in parts:
+        close(k, 1)
+        rings[k][3][2].open()
+    pltpu.make_async_copy(w_bytes, w_bytes, local_sems.at[16]).wait()
+    arrive(w_id, w_bytes)
     for k in parts:
         multiply(k, 0)
-    for step in (-1, 1, 2):
+        rings[k][2][2].relay()
+    for step in (1, -1, 2):
         for k in parts:
-            rings[k][2][step].relay()
+            rings[k][3][step].relay()
     for k in parts:
         multiply(k, -1)
         multiply(k, 1)
     for k in parts:
-        for step in (0, -1, 1, 2):
-            rings[k][2][step].close()
+        close(k, 2)
         multiply(k, 2)
 
     sub = lax.broadcasted_iota(jnp.int32, (32, ROWS, 128), 1)
@@ -292,10 +319,8 @@
     hidden = jnp.maximum(gate_value, 0.0) * up_value * jnp.where(low, wanted[0], wanted[1])
     hid[...] = hidden.astype(BF16).reshape(2, 4, 4, ROWS, 256)
 
-    for copy in weights[4:]:
-        copy.wait()
-    for i in range(2):
-        arrive(weight_ids[4 + i], d.at[i, pl.ds(pl.multiple_of((1 - core) * 128, 128), 128), :])
+    pltpu.make_async_copy(d_bytes, d_bytes, local_sems.at[17]).wait()
+    arrive(d_id, d_bytes)
 
     def terms(k, step, store):
         c = ORDERS[k][2]
@@ -332,123 +357,139 @@
                 ref[k, y, :, :, 0:width(k)] = value.astype(ref.dtype)
         return store
 
-    order = (2, 1, -1, 0)
-    ids = {}
-    for k in parts:
-        c = ORDERS[k][2]
-        one, two = cut(0, width(k))
-        terms(k, 2, fill(send_two, k))
-        for step in order:
-            ids[k, step, "two_plus"] = send(line(send_two, k, step, one), line(got_two_plus, k, step, one), along(c, 1))
-            ids[k, step, "two_minus"] = send(line(send_two, k, step, two), line(got_two_minus, k, step, two), along(c, -1))
-    for k in parts:
-        c = ORDERS[k][2]
-        one, two = cut(0, width(k))
-        terms(k, 1, fill(send_plus, k))
-        terms(k, -1, fill(send_minus, k))
-        for step in order:
-            ids[k, step, "plus_two"] = send(line(send_plus, k, step, two), line(got_plus, k, step, two), along(c, 1))
-            ids[k, step, "minus_one"] = send(line(send_minus, k, step, one), line(got_minus, k, step, one), along(c, -1))
-    for k in parts:
-        terms(k, 0, fill(total, k))
-
     def add_into(ref, *others):
         value = ref[...].astype(F32)
         for other in others:
             value = value + other[...].astype(F32)
         ref[...] = value.astype(ref.dtype)
 
-    for step in order:
+    def halves(k):
+        one, two = cut(0, width(k))
+        return slice(*one), slice(*two), slice(0, width(k))
+
+    ids = {(k, step, kind): arrival() for k in parts for step in around for kind in ("two", "sum")}
+    ids.update({(k, name): arrival() for k in parts for name in ("two", "sum", "unit_two", "unit_sum")})
+
+    def push(k, step, src, dst, columns, way, kind):
+        send(6, ids[k, step, kind], line(src, k, step, columns), line(dst, k, step, columns), along(ORDERS[k][2], way))
+
+    def push_plain(k, step):
+        one, two = cut(0, width(k))
+        push(k, step, send_plus, got_plus, two, 1, "sum")
+        push(k, step, send_minus, got_minus, one, -1, "sum")
+
+    def push_sums(k, step):
+        one, two = cut(0, width(k))
+        arrive(ids[k, step, "two"], line(got_plus, k, step))
+        add_into(line(send_plus, k, step, one), line(got_two_plus, k, step, one))
+        push(k, step, send_plus, got_plus, one, 1, "sum")
+        add_into(line(send_minus, k, step, two), line(got_two_minus, k, step, two))
+        push(k, step, send_minus, got_minus, two, -1, "sum")
+
+    def push_line(k, src, dst, columns, way, kind):
+        send(7, ids[k, kind], src.at[k, :, :, columns], dst.at[k, :, :, columns], along(ORDERS[k][1], way))
+
+    def finish(k, step):
+        one, two, full = halves(k)
+        arrive(ids[k, step, "sum"], got_plus.at[k, 0:2, :, :, full])
+        value = (line(total, k, step)[...] + line(got_plus, k, step)[...].astype(F32)
+                 + line(got_minus, k, step)[...].astype(F32))
+        if step == 2:
+            line_two[k, :, :, full] = value.astype(BF16)
+            push_line(k, line_two, line_got_two_plus, one, 1, "two")
+            push_line(k, line_two, line_got_two_minus, two, -1, "two")
+        elif step == 1:
+            line_plus[k, :, :, full] = value.astype(BF16)
+            push_line(k, line_plus, line_got_plus, two, 1, "sum")
+        elif step == -1:
+            line_minus[k, :, :, full] = value.astype(BF16)
+            push_line(k, line_minus, line_got_minus, one, -1, "sum")
+        else:
+            line(total, k, 0)[...] = value
+
+    def push_line_sums(k):
+        one, two, full = halves(k)
+        arrive(ids[k, "two"], line_got_plus.at[k, :, :, full])
+        add_into(line_plus.at[k, :, :, one], line_got_two_plus.at[k, :, :, one])
+        push_line(k, line_plus, line_got_plus, one, 1, "sum")
+        add_into(line_minus.at[k, :, :, two], line_got_two_minus.at[k, :, :, two])
+        push_line(k, line_minus, line_got_minus, two, -1, "sum")
+
+    for k in parts:
+        one, two = cut(0, width(k))
+        terms(k, 2, fill(send_two, k))
+        for step in (2, 1, -1, 0):
+            push(k, step, send_two, got_two_plus, one, 1, "two")
+            push(k, step, send_two, got_two_minus, two, -1, "two")
+    for k in parts:
+        terms(k, 1, fill(send_plus, k))
+        terms(k, -1, fill(send_minus, k))
+        push_plain(k, 2)
+    for k in parts:
+        terms(k, 0, fill(total, k))
+    for step, later in ((2, 1), (1, -1), (-1, 0)):
         for k in parts:
-            c = ORDERS[k][2]
-            one, two = cut(0, width(k))
-            arrive(ids[k, step, "two_plus"], line(got_two_plus, k, step, one))
-            add_into(line(send_plus, k, step, one), line(got_two_plus, k, step, one))
-            ids[k, step, "plus_one"] = send(line(send_plus, k, step, one), line(got_plus, k, step, one), along(c, 1))
-            arrive(ids[k, step, "two_minus"], line(got_two_minus, k, step, two))
-            add_into(line(send_minus, k, step, two), line(got_two_minus, k, step, two))
-            ids[k, step, "minus_two"] = send(line(send_minus, k, step, two), line(got_minus, k, step, two), along(c, -1))
-
-    for step in order:
+            push_sums(k, step)
         for k in parts:
-            b = ORDERS[k][1]
-            n = width(k)
-            one, two = cut(0, n)
-            one_s, two_s, all_s = slice(*one), slice(*two), slice(0, n)
-            arrive(ids[k, step, "plus_two"], line(got_plus, k, step, two))
-            arrive(ids[k, step, "plus_one"], line(got_plus, k, step, one))
-            arrive(ids[k, step, "minus_one"], line(got_minus, k, step, one))
-            arrive(ids[k, step, "minus_two"], line(got_minus, k, step, two))
-            value = (line(total, k, step)[...] + line(got_plus, k, step)[...].astype(F32)
-                     + line(got_minus, k, step)[...].astype(F32))
-            if step == 2:
-                line_two[k, :, :, all_s] = value.astype(BF16)
-                ids[k, "two_plus"] = send(
-                    line_two.at[k, :, :, one_s], line_got_two_plus.at[k, :, :, one_s], along(b, 1))
-                ids[k, "two_minus"] = send(
-                    line_two.at[k, :, :, two_s], line_got_two_minus.at[k, :, :, two_s], along(b, -1))
-            elif step == 1:
-                line_plus[k, :, :, all_s] = value.astype(BF16)
-                ids[k, "plus_two"] = send(
-                    line_plus.at[k, :, :, two_s], line_got_plus.at[k, :, :, two_s], along(b, 1))
-            elif step == -1:
-                line_minus[k, :, :, all_s] = value.astype(BF16)
-                ids[k, "minus_one"] = send(
-                    line_minus.at[k, :, :, one_s], line_got_minus.at[k, :, :, one_s], along(b, -1))
-            else:
-                line(total, k, 0)[...] = value
-            if step == -1:
-                arrive(ids[k, "two_plus"], line_got_two_plus.at[k, :, :, one_s])
-                add_into(line_plus.at[k, :, :, one_s], line_got_two_plus.at[k, :, :, one_s])
-                ids[k, "plus_one"] = send(
-                    line_plus.at[k, :, :, one_s], line_got_plus.at[k, :, :, one_s], along(b, 1))
-                arrive(ids[k, "two_minus"], line_got_two_minus.at[k, :, :, two_s])
-                add_into(line_minus.at[k, :, :, two_s], line_got_two_minus.at[k, :, :, two_s])
-                ids[k, "minus_two"] = send(
-                    line_minus.at[k, :, :, two_s], line_got_minus.at[k, :, :, two_s], along(b, -1))
+            push_plain(k, later)
+    for k in parts:
+        finish(k, 2)
+    for k in parts:
+        push_sums(k, 0)
+    for step in (1, -1):
+        for k in parts:
+            finish(k, step)
+    for k in parts:
+        push_line_sums(k)
+    for k in parts:
+        finish(k, 0)
+
+    def push_unit(k, src, dst, way, kind):
+        full = halves(k)[2]
+        send(8, ids[k, kind], src.at[k, :, full], dst.at[k, :, full], along(ORDERS[k][0], way))
 
     for k in parts:
         a = ORDERS[k][0]
-        n = width(k)
-        one, two = cut(0, n)
-        one_s, two_s, all_s = slice(*one), slice(*two), slice(0, n)
-        arrive(ids[k, "plus_two"], line_got_plus.at[k, :, :, two_s])
-        arrive(ids[k, "plus_one"], line_got_plus.at[k, :, :, one_s])
-        arrive(ids[k, "minus_one"], line_got_minus.at[k, :, :, one_s])
-        arrive(ids[k, "minus_two"], line_got_minus.at[k, :, :, two_s])
-        add_into(line(total, k, 0), line_got_plus.at[k, :, :, all_s], line_got_minus.at[k, :, :, all_s])
+        full = halves(k)[2]
+        arrive(ids[k, "sum"], got_plus.at[k, 0:2, :, :, full])
+        add_into(line(total, k, 0), line_got_plus.at[k, :, :, full], line_got_minus.at[k, :, :, full])
         whole = line(total, k, 0)
-        unit_two[k, :, all_s] = whole.at[near(a, 2)][...].astype(BF16)
-        ids[k, "unit_two"] = send(unit_two.at[k, :, all_s], unit_got_two.at[k, :, all_s], along(a, 1))
-        unit_minus[k, :, all_s] = whole.at[near(a, -1)][...].astype(BF16)
-        ids[k, "unit_minus"] = send(unit_minus.at[k, :, all_s], unit_got_minus.at[k, :, all_s], along(a, -1))
+        unit_two[k, :, full] = whole.at[near(a, 2)][...].astype(BF16)
+        push_unit(k, unit_two, unit_got_two, 1, "unit_two")
+        unit_minus[k, :, full] = whole.at[near(a, -1)][...].astype(BF16)
+        push_unit(k, unit_minus, unit_got_minus, -1, "unit_sum")
     for k in parts:
         a = ORDERS[k][0]
-        all_s = slice(0, width(k))
-        arrive(ids[k, "unit_two"], unit_got_two.at[k, :, all_s])
-        value = line(total, k, 0).at[near(a, 1)][...] + unit_got_two[k, :, all_s].astype(F32)
-        unit_plus[k, :, all_s] = value.astype(BF16)
-        ids[k, "unit_plus"] = send(unit_plus.at[k, :, all_s], unit_got_plus.at[k, :, all_s], along(a, 1))
+        full = halves(k)[2]
+        arrive(ids[k, "unit_two"], unit_got_two.at[k, :, full])
+        value = line(total, k, 0).at[near(a, 1)][...] + unit_got_two[k, :, full].astype(F32)
+        unit_plus[k, :, full] = value.astype(BF16)
+        push_unit(k, unit_plus, unit_got_plus, 1, "unit_sum")
+    last = arrival()
     kept = []
     for k in parts:
         a = ORDERS[k][0]
-        all_s = slice(0, width(k))
-        arrive(ids[k, "unit_minus"], unit_got_minus.at[k, :, all_s])
-        arrive(ids[k, "unit_plus"], unit_got_plus.at[k, :, all_s])
-        value = (line(total, k, 0).at[near(a, 0)][...] + unit_got_plus[k, :, all_s].astype(F32)
-                 + unit_got_minus[k, :, all_s].astype(F32))
+        full = halves(k)[2]
+        arrive(ids[k, "unit_sum"], got_plus.at[k, 0, 0:2, :, full])
+        value = (line(total, k, 0).at[near(a, 0)][...] + unit_got_plus[k, :, full].astype(F32)
+                 + unit_got_minus[k, :, full].astype(F32))
         value = stream[:, slice(*TERMS[k])] + value
-        kept.append(jnp.where(first, value[0:4], value[4:8]).astype(BF16))
+        kept.append(jnp.where(first, value[0:4], value[4:8]))
         to_tp[:, slice(*TERMS[k])] = jnp.where(first, value[4:8], value[0:4]).astype(BF16)
-    last = send(to_tp, from_tp, pair)
+    send(9, last, to_tp, from_tp, pair)
+    for group, src in (
+        (0, residual.at[:, 0:HALF]), (1, w_bytes), (2, d_bytes),
+        (3, g.at[0:3, 0, 0]), (4, g.at[0:3, 0]), (5, g.at[0:3]),
+        (6, g.at[0:3, :, :, :, 0:HALF]), (7, g.at[0:3, 0, :, :, 0:HALF]), (8, g.at[0:3, 0, 0, :, 0:HALF]),
+    ):
+        sent(group, src)
     arrive(last, from_tp)
     for k in parts:
         lo, hi = TERMS[k]
-        theirs = from_tp[:, lo:hi]
+        theirs = from_tp[:, lo:hi].astype(F32)
         out[:, lo:hi] = jnp.where(first, kept[k], theirs)
         out[:, HALF + lo:HALF + hi] = jnp.where(first, theirs, kept[k])
-    for copy in started:
-        copy.wait_send()
+    sent(9, to_tp)
 
 
 def shards(
@@ -462,7 +503,7 @@
     unit = (3, ROWS, 1408)
     return pl.pallas_call(
         kernel,
-        out_shape=jax.ShapeDtypeStruct((4, 8192), BF16),
+        out_shape=jax.ShapeDtypeStruct((4, 8192), F32),
         in_specs=[pl.BlockSpec(memory_space=pltpu.SMEM)] + [vmem] * 6 + [hbm] * 5,
         out_specs=vmem,
         scratch_shapes=[
@@ -486,14 +527,14 @@
         + [pltpu.VMEM(rows, BF16)] * 7
         + [pltpu.VMEM(unit, BF16)] * 6
         + [
-            pltpu.SemaphoreType.DMA((COPIES,)),
-            pltpu.SemaphoreType.DMA((COPIES,)),
-            pltpu.SemaphoreType.DMA((32,)),
+            pltpu.SemaphoreType.DMA((SENDS,)),
+            pltpu.SemaphoreType.DMA((ARRIVALS,)),
+            pltpu.SemaphoreType.DMA((FETCHES,)),
         ],
         compiler_params=pltpu.CompilerParams(
             collective_id=0, has_side_effects=True, vmem_limit_bytes=60 * 2**20),
     )(cache_lengths, queries, new_keys, token_values, residual, norm_gain.reshape(1, 8192), active,
-      key_cache, stored_values, gate_weight, up_weight, down_weight)
+      key_cache, stored_values, gate_weight, up_weight, down_weight).astype(BF16)
 
 
 def solution(mesh):

time: 75.4 us -> 65.2 us (0.86); the launches traced: 74.5 us -> 65.1 us
  Pallas kernels: 73 us -> 63.5 us
  other arithmetic: 0 us -> 1.56 us
  local copies, waits for them, and re-layouts: 1.49 us -> 0 us
    pallas_call x1, Pallas kernels: 73 us -> 63.5 us  [shards(): pl.pallas_call(kernel, out_shape=jax.ShapeDtypeStruct((4, 8192), F32), in...]
    convert_element_type x0 -> x1, other arithmetic: none -> 1.56 us  [shards(): return pl.pallas_call(kernel, out_shape=jax.ShapeDtypeStruct((4, 8192), F...]
    unnamed x1 -> x0, local copies, waits for them, and re-layouts: 1.49 us -> none
where the time goes in v3:
time: 65.2 us; the launch traced here: 65.1 us
  Pallas kernels  63.5 us (97%)
  other arithmetic  1.56 us (2%)
    pallas_call x1, Pallas kernels, shards(): pl.pallas_call(kernel, out_shape=jax.ShapeDtypeStruct((4, 8192), F32), in...  63.5 us
    convert_element_type x1, other arithmetic, shards(): return pl.pallas_call(kernel, out_shape=jax.ShapeDtypeStruct((4, 8192), F...  1.56 us

profile of v3, /device:TPU:0, one launch (start us, length us, event | category | flops | bytes accessed | tf_op | source)
XLA Modules:
  0.0 65.1 jit_solution(9731994094993730460)
XLA Ops:
  0.0 63.5 %shard_map.118 = f32[4,8192]{1,0:T(4,128)} custom-call(s32[8]{0:T(128)} %lengths.1, bf16[8,4096]{1,0:T(8,128)(2,1)} %queries.1, bf16[8,512]{1,0:T(8,128)(2,1)} %new_keys.1, bf16[8,512]{1,0:T(8,128)(2,1)} %token_values.1, bf16[4,8192]{1,0:T(4,128)(2,1)} %residual.1, f32[1,8192]{1,0:T(1,128)} %bitcast.1, s32[4,16]{1,0:T(4,128)} %active.1, ...), custom_call_target="tpu_custom_call" | custom-call | tf_op jit(solution)/shard_map/pallas_call | solution.py:504
  63.5 1.6 %convert_element_type.3 = bf16[4,8192]{1,0:T(4,128)(2,1)} convert(f32[4,8192]{1,0:T(4,128)} %shard_map.118) | non-fusion elementwise | flops 32768 | bytes 196608 | tf_op jit(solution)/shard_map/convert_element_type | solution.py:537

commit v4 on v3

--- a/solution.py
+++ b/solution.py
@@ -19,8 +19,8 @@
 TERMS = ((0, 1408), (1408, 2816), (2816, 4096))
 ORDERS = (("x", "y", "z"), ("y", "z", "x"), ("z", "x", "y"))
 SENDS = 10
-ARRIVALS = 128
-FETCHES = 18
+ARRIVALS = 139
+FETCHES = 25
 
 
 def cut(lo, hi):
@@ -29,9 +29,10 @@
 
 
 def kernel(
-    lengths, queries, new_keys, token_values, residual, gain, active,
+    lengths_in, queries_in, new_keys_in, token_values_in, residual_in, gain_in, active_in,
     key_cache, stored_values, gate, up, down,
     out,
+    lengths, queries, new_keys, token_values, residual, gain, active,
     keys, values, w, d, g, acc, hid, stream, scores, probs, blend, other_resid, to_tp, from_tp,
     send_two, send_plus, send_minus, got_two_plus, got_two_minus, got_plus, got_minus, total,
     line_two, line_plus, line_minus, line_got_two_plus, line_got_two_minus, line_got_plus, line_got_minus,
@@ -82,6 +83,9 @@
         copy.start()
         return copy
 
+    small = [fetch(src, dst, 18 + n) for n, (src, dst) in enumerate((
+        (lengths_in, lengths), (queries_in, queries), (new_keys_in, new_keys), (token_values_in, token_values),
+        (residual_in, residual), (gain_in, gain), (active_in, active)))]
     key_rows = [fetch(key_cache.at[r], keys.at[r], r) for r in range(ROWS)]
     value_rows = [fetch(stored_values.at[r], values.at[r], ROWS + r) for r in range(ROWS)]
     mine = pl.ds(pl.multiple_of(core * 128, 128), 128)
@@ -105,9 +109,12 @@
 
     theirs_half = pl.ds(pl.multiple_of((1 - tp) * HALF, 128), HALF)
     resid_id, w_id, d_id = arrival(), arrival(), arrival()
-    send(0, resid_id, residual.at[:, theirs_half], other_resid, pair)
+    send(0, resid_id, residual_in.at[:, theirs_half], other_resid, pair)
     for n, (src, dst) in enumerate(pieces):
         send(1 + n // 4, (w_id, d_id)[n // 4], src, dst, twin)
+
+    for copy in small:
+        copy.wait()
 
     first = tp == 0
     scale = 128 ** (-0.5)
@@ -163,6 +170,8 @@
                 [jnp.where(first, own, other), jnp.where(first, other, own)], axis=0)
             value = resid + block[i * 8:(i + 1) * 8]
             stream[:, lo:lo + 128] = value
+            part = block[i * 8:(i + 1) * 8]
+            to_tp[:, lo:lo + 128] = jnp.where(first, part[4:8], part[0:4]).astype(BF16)
             squares = squares + value * value
             factor = jnp.where(first, gain[:, lo:lo + 128], gain[:, HALF + lo:HALF + lo + 128])
             g[me + (slice(None), slice(lo, lo + 128))] = (value * factor).astype(BF16)
@@ -253,6 +262,8 @@
     for phase in range(3):
         for k in parts:
             (rings[k][0] if phase == 0 else rings[k][phase][0]).open()
+    context_id = arrival()
+    send(9, context_id, to_tp, from_tp, pair)
     acc[...] = jnp.zeros_like(acc)
     for k in parts:
         rings[k][0].relay()
@@ -329,25 +340,32 @@
         n = TERMS[k][1] - TERMS[k][0]
         if c == "y":
             rows = hid[at // 2].reshape(128, 256)
-            part = jnp.dot(rows, d[lax.rem(at, 2), :, columns], preferred_element_type=F32)
-            store(slice(None), part.reshape(4, 4, ROWS, n))
+        else:
+            rows = (hid[:, at] if c == "z" else hid[:, :, at]).reshape(64, 256)
+        one, two = [
+            jnp.dot(rows, d[t, :, columns], preferred_element_type=F32).reshape(-1, ROWS, n) for t in range(2)]
+        above = lax.broadcasted_iota(jnp.int32, one.shape, 1) < 4
+        crossed = pltpu.roll(jnp.where(above, two, one), 4, 1)
+        if c == "y":
+            even = lax.rem(at, 2) == 0
+            value = jnp.where(above, jnp.where(even, one, crossed), jnp.where(even, crossed, two))
+            store(slice(None), value.reshape(4, 4, ROWS, n))
             return
-        rows = (hid[:, at] if c == "z" else hid[:, :, at]).reshape(64, 256)
-        for t in range(2):
-            part = jnp.dot(rows, d[t, :, columns], preferred_element_type=F32).reshape(2, 4, ROWS, n)
-            store(t, part[0])
-            store(2 + t, part[1])
+        for t, value in enumerate((jnp.where(above, one, crossed), jnp.where(above, crossed, two))):
+            value = value.reshape(2, 4, ROWS, n)
+            store(t, value[0])
+            store(2 + t, value[1])
 
     def width(k):
         return TERMS[k][1] - TERMS[k][0]
 
-    def line(ref, k, step, columns=None):
+    def line(ref, k, piece, columns=None):
         a, b, c = ORDERS[k]
+        step, across = piece if isinstance(piece, tuple) else (piece, None)
         at = near(b, step)
+        across = slice(None) if across is None else near(a, across)
         columns = slice(0, width(k)) if columns is None else slice(*columns)
-        lead = (at,) if b == "y" else (slice(None), at)
-        rest = (slice(None),) if b == "y" else ()
-        return ref.at[(k,) + lead + rest + (slice(None), columns)]
+        return ref.at[(k,) + ((at, across) if b == "y" else (across, at)) + (slice(None), columns)]
 
     def fill(ref, k):
         def store(y, value):
@@ -367,7 +385,9 @@
         one, two = cut(0, width(k))
         return slice(*one), slice(*two), slice(0, width(k))
 
-    ids = {(k, step, kind): arrival() for k in parts for step in around for kind in ("two", "sum")}
+    own = [(0, 2), (0, 1), (0, -1), (0, 0)]
+    pieces = [2, 1, -1] + own
+    ids = {(k, piece, kind): arrival() for k in parts for piece in pieces for kind in ("two", "sum")}
     ids.update({(k, name): arrival() for k in parts for name in ("two", "sum", "unit_two", "unit_sum")})
 
     def push(k, step, src, dst, columns, way, kind):
@@ -391,7 +411,8 @@
 
     def finish(k, step):
         one, two, full = halves(k)
-        arrive(ids[k, step, "sum"], got_plus.at[k, 0:2, :, :, full])
+        single = isinstance(step, tuple)
+        arrive(ids[k, step, "sum"], got_plus.at[(k,) + ((0,) if single else ()) + (slice(0, 2),) + ((slice(None),) * (1 if single else 2)) + (full,)])
         value = (line(total, k, step)[...] + line(got_plus, k, step)[...].astype(F32)
                  + line(got_minus, k, step)[...].astype(F32))
         if step == 2:
@@ -405,7 +426,7 @@
             line_minus[k, :, :, full] = value.astype(BF16)
             push_line(k, line_minus, line_got_minus, one, -1, "sum")
         else:
-            line(total, k, 0)[...] = value
+            line(total, k, step)[...] = value
 
     def push_line_sums(k):
         one, two, full = halves(k)
@@ -418,7 +439,7 @@
     for k in parts:
         one, two = cut(0, width(k))
         terms(k, 2, fill(send_two, k))
-        for step in (2, 1, -1, 0):
+        for step in pieces:
             push(k, step, send_two, got_two_plus, one, 1, "two")
             push(k, step, send_two, got_two_minus, two, -1, "two")
     for k in parts:
@@ -427,69 +448,75 @@
         push_plain(k, 2)
     for k in parts:
         terms(k, 0, fill(total, k))
-    for step, later in ((2, 1), (1, -1), (-1, 0)):
+    for now, later in (([2], [1]), ([1], [-1]), ([-1], own[:2])):
         for k in parts:
-            push_sums(k, step)
+            for piece in now:
+                push_sums(k, piece)
         for k in parts:
-            push_plain(k, later)
+            for piece in later:
+                push_plain(k, piece)
     for k in parts:
         finish(k, 2)
     for k in parts:
-        push_sums(k, 0)
-    for step in (1, -1):
-        for k in parts:
-            finish(k, step)
+        push_sums(k, own[0])
+        push_sums(k, own[1])
+    for k in parts:
+        push_plain(k, own[2])
+        push_plain(k, own[3])
+    for k in parts:
+        finish(k, 1)
+    for k in parts:
+        push_sums(k, own[2])
+        push_sums(k, own[3])
+    for k in parts:
+        finish(k, -1)
     for k in parts:
         push_line_sums(k)
-    for k in parts:
-        finish(k, 0)
 
     def push_unit(k, src, dst, way, kind):
         full = halves(k)[2]
         send(8, ids[k, kind], src.at[k, :, full], dst.at[k, :, full], along(ORDERS[k][0], way))
 
-    for k in parts:
+    def unit_sum(k, piece):
         a = ORDERS[k][0]
         full = halves(k)[2]
+        finish(k, piece)
+        at = near(a, piece[1])
+        return (line(total, k, piece)[...] + line_got_plus[k, at, :, full].astype(F32)
+                + line_got_minus[k, at, :, full].astype(F32))
+
+    for k in parts:
+        full = halves(k)[2]
         arrive(ids[k, "sum"], got_plus.at[k, 0:2, :, :, full])
-        add_into(line(total, k, 0), line_got_plus.at[k, :, :, full], line_got_minus.at[k, :, :, full])
-        whole = line(total, k, 0)
-        unit_two[k, :, full] = whole.at[near(a, 2)][...].astype(BF16)
+        unit_two[k, :, full] = unit_sum(k, own[0]).astype(BF16)
         push_unit(k, unit_two, unit_got_two, 1, "unit_two")
-        unit_minus[k, :, full] = whole.at[near(a, -1)][...].astype(BF16)
+    for k in parts:
+        full = halves(k)[2]
+        value = unit_sum(k, own[1])
+        arrive(ids[k, "unit_two"], unit_got_two.at[k, :, full])
+        unit_plus[k, :, full] = (value + unit_got_two[k, :, full].astype(F32)).astype(BF16)
+        push_unit(k, unit_plus, unit_got_plus, 1, "unit_sum")
+        unit_minus[k, :, full] = unit_sum(k, own[2]).astype(BF16)
         push_unit(k, unit_minus, unit_got_minus, -1, "unit_sum")
-    for k in parts:
-        a = ORDERS[k][0]
-        full = halves(k)[2]
-        arrive(ids[k, "unit_two"], unit_got_two.at[k, :, full])
-        value = line(total, k, 0).at[near(a, 1)][...] + unit_got_two[k, :, full].astype(F32)
-        unit_plus[k, :, full] = value.astype(BF16)
-        push_unit(k, unit_plus, unit_got_plus, 1, "unit_sum")
-    last = arrival()
-    kept = []
-    for k in parts:
-        a = ORDERS[k][0]
-        full = halves(k)[2]
-        arrive(ids[k, "unit_sum"], got_plus.at[k, 0, 0:2, :, full])
-        value = (line(total, k, 0).at[near(a, 0)][...] + unit_got_plus[k, :, full].astype(F32)
-                 + unit_got_minus[k, :, full].astype(F32))
-        value = stream[:, slice(*TERMS[k])] + value
-        kept.append(jnp.where(first, value[0:4], value[4:8]))
-        to_tp[:, slice(*TERMS[k])] = jnp.where(first, value[4:8], value[0:4]).astype(BF16)
-    send(9, last, to_tp, from_tp, pair)
+    arrive(context_id, from_tp)
+    sums = [unit_sum(k, own[3]) for k in parts]
     for group, src in (
         (0, residual.at[:, 0:HALF]), (1, w_bytes), (2, d_bytes),
-        (3, g.at[0:3, 0, 0]), (4, g.at[0:3, 0]), (5, g.at[0:3]),
-        (6, g.at[0:3, :, :, :, 0:HALF]), (7, g.at[0:3, 0, :, :, 0:HALF]), (8, g.at[0:3, 0, 0, :, 0:HALF]),
+        (3, g.at[0:3, 0, 0]), (4, g.at[0:3, 0]), (5, g.at[0:3]), (9, to_tp),
+        (6, g.at[0:3, :, :, :, 0:HALF]), (7, g.at[0:3, 0, :, :, 0:HALF]),
     ):
         sent(group, src)
-    arrive(last, from_tp)
     for k in parts:
         lo, hi = TERMS[k]
-        theirs = from_tp[:, lo:hi].astype(F32)
-        out[:, lo:hi] = jnp.where(first, kept[k], theirs)
-        out[:, HALF + lo:HALF + hi] = jnp.where(first, theirs, kept[k])
-    sent(9, to_tp)
+        full = halves(k)[2]
+        ours = jnp.where(first, stream[0:4, lo:hi], stream[4:8, lo:hi])
+        theirs = jnp.where(first, residual[:, HALF + lo:HALF + hi], residual[:, lo:hi]).astype(F32)
+        theirs = theirs + from_tp[:, lo:hi].astype(F32)
+        arrive(ids[k, "unit_sum"], got_plus.at[k, 0, 0:2, :, full])
+        value = sums[k] + unit_got_plus[k, :, full].astype(F32) + unit_got_minus[k, :, full].astype(F32)
+        out[:, lo:hi] = value[0:4] + jnp.where(first, ours, theirs)
+        out[:, HALF + lo:HALF + hi] = value[4:8] + jnp.where(first, theirs, ours)
+    sent(8, g.at[0:3, 0, 0, :, 0:HALF])
 
 
 def shards(
@@ -497,16 +524,23 @@
     active, gate_weight, up_weight, down_weight,
 ):
     vmem = pl.BlockSpec(memory_space=pltpu.VMEM)
-    hbm = pl.BlockSpec(memory_space=pl.ANY)
+    hbm = pl.BlockSpec(memory_space=pltpu.HBM)
     slab = (3, 4, 4, ROWS, 1408)
     rows = (3, 4, ROWS, 1408)
     unit = (3, ROWS, 1408)
     return pl.pallas_call(
         kernel,
         out_shape=jax.ShapeDtypeStruct((4, 8192), F32),
-        in_specs=[pl.BlockSpec(memory_space=pltpu.SMEM)] + [vmem] * 6 + [hbm] * 5,
+        in_specs=[hbm] * 12,
         out_specs=vmem,
         scratch_shapes=[
+            pltpu.SMEM((ROWS,), jnp.int32),
+            pltpu.VMEM((ROWS, HALF), BF16),
+            pltpu.VMEM((ROWS, 512), BF16),
+            pltpu.VMEM((ROWS, 512), BF16),
+            pltpu.VMEM((4, 8192), BF16),
+            pltpu.VMEM((1, 8192), F32),
+            pltpu.VMEM((4, 16), jnp.int32),
             pltpu.VMEM((ROWS, 256, 512), BF16),
             pltpu.VMEM((ROWS, 256, 512), BF16),
             pltpu.VMEM((2, HALF, 512), BF16),
@@ -532,9 +566,10 @@
             pltpu.SemaphoreType.DMA((FETCHES,)),
         ],
         compiler_params=pltpu.CompilerParams(
-            collective_id=0, has_side_effects=True, vmem_limit_bytes=60 * 2**20),
-    )(cache_lengths, queries, new_keys, token_values, residual, norm_gain.reshape(1, 8192), active,
-      key_cache, stored_values, gate_weight, up_weight, down_weight).astype(BF16)
+            collective_id=0, has_side_effects=True, vmem_limit_bytes=48 * 2**20),
+    )(*[pltpu.with_memory_space_constraint(array, pltpu.HBM) for array in (
+        cache_lengths, queries, new_keys, token_values, residual, norm_gain.reshape(1, 8192), active,
+        key_cache, stored_values, gate_weight, up_weight, down_weight)]).astype(BF16)
 
 
 def solution(mesh):

time: 65.2 us -> 60.4 us (0.926)
  Pallas kernels: 63.5 us -> 59.7 us
  other arithmetic: 1.56 us -> 0.65 us
    pallas_call x1, Pallas kernels: 63.5 us -> 59.7 us  [shards(): pl.pallas_call(kernel, out_shape=jax.ShapeDtypeStruct((4, 8192), F32), in...]
    convert_element_type x1, other arithmetic: 1.56 us -> 0.65 us  [shards(): return pl.pallas_call(kernel, out_shape=jax.ShapeDtypeStruct((4, 8192), F...]
where the time goes in v4:
time: 60.4 us; the launch traced here: 60.3 us
  Pallas kernels  59.7 us (99%)
  other arithmetic  0.65 us (1%)
    pallas_call x1, Pallas kernels, shards(): pl.pallas_call(kernel, out_shape=jax.ShapeDtypeStruct((4, 8192), F32), in...  59.7 us

profile of v4, /device:TPU:0, one launch (start us, length us, event | category | flops | bytes accessed | tf_op | source)
XLA Modules:
  0.0 60.3 jit_solution(9689006628154056789)
XLA Ops:
  0.0 59.7 %shard_map.118 = f32[4,8192]{1,0:T(4,128)S(1)} custom-call(s32[8]{0:T(128)} %lengths_in.1, bf16[8,4096]{1,0:T(8,128)(2,1)} %queries_in.1, bf16[8,512]{1,0:T(8,128)(2,1)} %new_keys_in.1, bf16[8,512]{1,0:T(8,128)(2,1)} %token_values_in.1, bf16[4,8192]{1,0:T(4,128)(2,1)} %residual_in.1, f32[1,8192]{1,0:T(1,128)} %bitcast.1, s32[4,16]{1,0:T(4,128)} %active_in.1, ...), custom_call_target="tpu_custom_call" | custom-call | tf_op jit(solution)/shard_map/pallas_call | solution.py:531
  59.7 0.7 %convert_element_type.3 = bf16[4,8192]{1,0:T(4,128)(2,1)} convert(f32[4,8192]{1,0:T(4,128)S(1)} %shard_map.118) | non-fusion elementwise | flops 32768 | bytes 196608 | tf_op jit(solution)/shard_map/convert_element_type | solution.py:572

commit v5 on v4

--- a/solution.py
+++ b/solution.py
@@ -126,13 +126,17 @@
     for j in range(4):
         grouped.append(jnp.concatenate(
             [queries[:, (j * 8 + i) * 128:(j * 8 + i + 1) * 128].astype(F32) for i in range(8)], axis=0))
-    for r in range(ROWS):
-        key_rows[r].wait()
+    masks = [jnp.broadcast_to(jnp.where(row_of == r, 1.0, 0.0), (64, 128)).astype(BF16) for r in range(ROWS)]
+    for part in (range(0, 4), range(4, 8)):
+        for r in part:
+            key_rows[r].wait()
         for j in range(4):
+            asked = grouped[j].astype(BF16)
             s = lax.dot_general(
-                grouped[j].astype(BF16), keys[r, :, j * 128:(j + 1) * 128], (((1,), (1,)), ((), ())),
-                preferred_element_type=F32)
-            scores[j] = s if r == 0 else jnp.where(row_of == r, s, scores[j])
+                jnp.concatenate([asked * masks[r] for r in part], axis=1),
+                jnp.concatenate([keys[r, :, j * 128:(j + 1) * 128] for r in part], axis=1),
+                (((1,), (1,)), ((), ())), preferred_element_type=F32)
+            scores[j] = s if part[0] == 0 else scores[j] + s
     column = lax.broadcasted_iota(jnp.int32, (64, 256), 1)
     fresh_probs = []
     for j in range(4):
@@ -143,13 +147,17 @@
         e = jnp.exp(s - highest)
         fresh_e = jnp.exp(fresh - highest)
         denominator = jnp.sum(e, axis=1, keepdims=True) + fresh_e
-        probs[j] = (e / denominator).astype(BF16)
-        fresh_probs.append((fresh_e / denominator).astype(BF16).astype(F32))
+        share = 1.0 / denominator
+        probs[j] = (e * share).astype(BF16)
+        fresh_probs.append((fresh_e * share).astype(BF16).astype(F32))
     for r in range(ROWS):
         value_rows[r].wait()
-        for j in range(4):
-            o = jnp.dot(probs[j], values[r, :, j * 128:(j + 1) * 128], preferred_element_type=F32)
-            blend[j] = o if r == 0 else jnp.where(row_of == r, o, blend[j])
+    for j in range(4):
+        shares = probs[j]
+        blend[j] = jnp.dot(
+            jnp.concatenate([shares * jnp.concatenate([masks[r]] * 2, axis=1) for r in range(ROWS)], axis=1),
+            jnp.concatenate([values[r, :, j * 128:(j + 1) * 128] for r in range(ROWS)], axis=0),
+            preferred_element_type=F32)
 
     lane = lax.broadcasted_iota(jnp.int32, (4, 128), 1)
     named = jnp.zeros((4, 128), F32)

time: 60.4 us -> 59.2 us (0.980)
  Pallas kernels: 59.7 us -> 58.4 us
    pallas_call x1, Pallas kernels: 59.7 us -> 58.4 us  [shards(): pl.pallas_call(kernel, out_shape=jax.ShapeDtypeStruct((4, 8192), F32), in...]
where the time goes in v5:
time: 59.2 us; the launch traced here: 59.1 us
  Pallas kernels  58.4 us (99%)
  other arithmetic  0.65 us (1%)
    pallas_call x1, Pallas kernels, shards(): pl.pallas_call(kernel, out_shape=jax.ShapeDtypeStruct((4, 8192), F32), in...  58.4 us

profile of v5, /device:TPU:0, one launch (start us, length us, event | category | flops | bytes accessed | tf_op | source)
XLA Modules:
  0.0 59.1 jit_solution(17506776775962295415)
XLA Ops:
  0.0 58.4 %shard_map.118 = f32[4,8192]{1,0:T(4,128)S(1)} custom-call(s32[8]{0:T(128)} %lengths_in.1, bf16[8,4096]{1,0:T(8,128)(2,1)} %queries_in.1, bf16[8,512]{1,0:T(8,128)(2,1)} %new_keys_in.1, bf16[8,512]{1,0:T(8,128)(2,1)} %token_values_in.1, bf16[4,8192]{1,0:T(4,128)(2,1)} %residual_in.1, f32[1,8192]{1,0:T(1,128)} %bitcast.1, s32[4,16]{1,0:T(4,128)} %active_in.1, ...), custom_call_target="tpu_custom_call" | custom-call | tf_op jit(solution)/shard_map/pallas_call | solution.py:539
  58.4 0.7 %convert_element_type.3 = bf16[4,8192]{1,0:T(4,128)(2,1)} convert(f32[4,8192]{1,0:T(4,128)S(1)} %shard_map.118) | non-fusion elementwise | flops 32768 | bytes 196608 | tf_op jit(solution)/shard_map/convert_element_type | solution.py:580
